TPU v7x, 128 devices: a whole 4x4x4 slice. The times are simulated.
128 devices in a mesh: dp: 16 (over z, y), mp: 8 (over x, core).
Axes of the slice: x: 4, y: 4, z: 4, core: 2. Of those that a mesh axis runs over, the one named last changes fastest.
Arguments:
- residual: bfloat16 [2048, 4096], P('dp', 'mp'), may hold values from -18 to 18
- queries: bfloat16 [2048, 4096], P('dp', 'mp'), may hold values from -20 to 20
- new_keys: bfloat16 [2048, 1024], P('dp', 'mp'), may hold values from -6 to 6
- new_values: bfloat16 [2048, 1024], P('dp', 'mp'), may hold values from -6 to 6
- cache_keys: bfloat16 [2048, 16, 1024], P('dp', None, 'mp'), may hold values from -6 to 6
- cache_values: bfloat16 [2048, 16, 1024], P('dp', None, 'mp'), may hold values from -6 to 6
- cache_len: int32 [1024], replicated, may hold values from 1 to 128, 16384 in all
- page_order: int32 [2048], replicated, may hold values from 0 to 2047, each once
- out_proj: bfloat16 [4096, 4096], P('mp'), may hold values from -0.09375 to 0.09375
- attn_gain: float32 [4096], replicated, may hold values from 0.25 to 1.75
- routes: int32 [2048, 2], P('dp'), may hold values from 0 to 7, all different within a row; in each aligned block of 128 rows (0 to 127, 128 to 255, ...) at most 48 rows name the same one
- route_weight: float32 [2048, 2], P('dp'), may hold values from 0.1 to 1
- gate_proj: bfloat16 [4096, 98304], P(None, ('dp', 'mp')), may hold values from -0.09375 to 0.09375
- up_proj: bfloat16 [4096, 98304], P(None, ('dp', 'mp')), may hold values from -0.09375 to 0.09375
- down_proj: bfloat16 [98304, 4096], P(('dp', 'mp')), may hold values from -0.0546875 to 0.0546875
- final_gain: float32 [4096], P('mp'), may hold values from 0.25 to 1.75
Outputs:
- layer_out: bfloat16 [2048, 4096], P('dp', 'mp')
Inputs may be any that keep to these rules, and one draw needn't show every extreme that they name: `routes`: in each aligned block of 128 rows (the rows of one dp group) no expert is named by more than 48 rows, a bound that some block reaches; a row's two experts differ. `cache_len`: the lengths sum to 16384, and the longest is exactly 128. `page_order`: each page number appears once; pages past the last request's are unused.
All inputs are finite; a program needn't handle non-finite values.
Results may differ from a plain program's by a relative error of at most 0.008.
Values may be sent and summed in bfloat16 or wider, within the bound.
A program may use at most 128 MiB of HBM per device.

v0:
```python
import jax
import jax.numpy as jnp
from jax import lax
from jax.sharding import PartitionSpec as P

D = 4096
HQ = 32
KVH = 8
HD = 128
E = 8
PAGE = 16
DEC = 64
PRE = 64
C = 48


neg_big = -1e30
eps_norm = 1e-05


def page_owner(page_ids, page_order, cache_len):
    page_count = (cache_len + PAGE - 1) // PAGE
    page_ends = jnp.cumsum(page_count)
    page_first = page_ends - page_count
    pool_iota = lax.broadcasted_iota(jnp.int32, (1, page_order.shape[0]), 1)
    order_pos = jnp.sum(jnp.where(page_order[None, :] == page_ids[:, None], pool_iota, 0), axis=1)
    owners = jnp.sum((page_ends[None, :] <= order_pos[:, None]).astype(jnp.int32), axis=1)
    request_iota = lax.broadcasted_iota(jnp.int32, (1, cache_len.shape[0]), 1)
    chosen = request_iota == owners[:, None]
    first_own = jnp.sum(jnp.where(chosen, page_first[None, :], 0), axis=1)
    length_own = jnp.sum(jnp.where(chosen, cache_len[None, :], 0), axis=1)
    offsets = lax.broadcasted_iota(jnp.int32, (1, PAGE), 1)
    key_pos = (order_pos - first_own)[:, None] * PAGE + offsets
    return (owners, key_pos < length_own[:, None])


def page_partials(page_queries, key_pages, value_pages, key_ok, scale):
    scores = (
        jnp.einsum("pkgh,pokh->pkgo", page_queries, key_pages, preferred_element_type=jnp.float32)
        * scale
    )
    wide_mask = key_ok[:, None, None, :]
    masked = jnp.where(wide_mask, scores, neg_big)
    maxima = jnp.max(masked, axis=3)
    weights = jnp.where(wide_mask, jnp.exp(masked - maxima[..., None]), 0.0)
    totals = jnp.sum(weights, axis=3)
    weighted = jnp.einsum(
        "pkgo,pokh->pkgh",
        weights,
        value_pages.astype(jnp.float32),
        precision=lax.Precision.HIGHEST,
        preferred_element_type=jnp.float32,
    )
    return (maxima, totals, weighted)


def fold_pages(maxima, totals, weighted, owned, local_owner):
    top_score = jnp.max(jnp.where(owned[:, :, None, None], maxima[:, None], neg_big), axis=0)
    page_top = top_score[local_owner]
    factors = jnp.exp(maxima - page_top)
    owned_float = owned.astype(jnp.float32)
    sums = jnp.einsum("pr,pkg->rkg", owned_float, totals * factors, precision=lax.Precision.HIGHEST)
    values = jnp.einsum(
        "pr,pkgh->rkgh", owned_float, weighted * factors[..., None], precision=lax.Precision.HIGHEST
    )
    return (top_score, sums, values)


def local(
    residual,
    queries,
    new_keys,
    new_values,
    cache_keys,
    cache_values,
    cache_len,
    page_order,
    out_proj,
    attn_gain,
    routes,
    route_weight,
    gate_proj,
    up_proj,
    down_proj,
    final_gain,
):
    dp_count = lax.axis_size("dp")
    dp_index = lax.axis_index("dp")
    mp_index = lax.axis_index("mp")
    scale = HD ** (-0.5)
    kv_local = new_keys.shape[1] // HD
    group_size = HQ // KVH
    width_local = residual.shape[1]
    pool_local = cache_keys.shape[0]
    request_total = cache_len.shape[0]
    query_heads = queries[:DEC].reshape(DEC, kv_local, group_size, HD)
    gathered = lax.all_gather(queries[:DEC], "dp", axis=0, tiled=True)
    gathered_heads = gathered.reshape(request_total, kv_local, group_size, HD)
    page_ids = dp_index * pool_local + lax.broadcasted_iota(jnp.int32, (pool_local,), 0)
    owners, key_ok = page_owner(page_ids, page_order, cache_len)
    live = owners < request_total
    local_owner = jnp.minimum(owners, request_total - 1)
    key_ok = key_ok & live[:, None]
    key_pages = cache_keys.reshape(pool_local, PAGE, kv_local, HD)
    value_pages = cache_values.reshape(pool_local, PAGE, kv_local, HD)
    page_queries = gathered_heads[local_owner]
    maxima, totals, weighted = page_partials(page_queries, key_pages, value_pages, key_ok, scale)
    owned = (local_owner[:, None] == lax.broadcasted_iota(jnp.int32, (1, request_total), 1)) & live[
        :, None
    ]
    maxima, totals, weighted = fold_pages(maxima, totals, weighted, owned, local_owner)
    maxima = maxima.reshape(dp_count, DEC, kv_local, group_size)
    totals = totals.reshape(dp_count, DEC, kv_local, group_size)
    weighted = weighted.reshape(dp_count, DEC, kv_local, group_size, HD)
    maxima, totals, weighted = (
        lax.all_to_all(maxima, "dp", split_axis=0, concat_axis=0, tiled=True),
        lax.all_to_all(totals, "dp", split_axis=0, concat_axis=0, tiled=True),
        lax.all_to_all(weighted, "dp", split_axis=0, concat_axis=0, tiled=True),
    )
    top_cache = jnp.max(maxima, axis=0)
    factors = jnp.exp(maxima - top_cache[None])
    cache_state = (
        top_cache,
        jnp.sum(totals * factors, axis=0),
        jnp.sum(weighted * factors[..., None], axis=0),
    )
    self_keys = new_keys[:DEC].reshape(DEC, kv_local, HD)
    self_values = new_values[:DEC].reshape(DEC, kv_local, HD).astype(jnp.float32)
    self_score = (
        jnp.einsum("rkgh,rkh->rkg", query_heads, self_keys, preferred_element_type=jnp.float32)
        * scale
    )
    cache_top, cache_total, cache_sum = cache_state
    top_score = jnp.maximum(cache_top, self_score)
    cache_factor = jnp.exp(cache_top - top_score)
    self_factor = jnp.exp(self_score - top_score)
    numerator = (
        cache_sum * cache_factor[..., None] + self_factor[..., None] * self_values[:, :, None, :]
    )
    denominator = cache_total * cache_factor + self_factor
    decode_out = (numerator / denominator[..., None]).astype(jnp.bfloat16).reshape(DEC, -1)
    prompt_q = queries[DEC:].reshape(PRE, kv_local, group_size, HD)
    prompt_k = new_keys[DEC:].reshape(PRE, kv_local, HD)
    prompt_v = new_values[DEC:].reshape(PRE, kv_local, HD).astype(jnp.float32)
    prompt_scores = (
        jnp.einsum("qkgh,tkh->kgqt", prompt_q, prompt_k, preferred_element_type=jnp.float32) * scale
    )
    causal = lax.broadcasted_iota(jnp.int32, (PRE, PRE), 0) >= lax.broadcasted_iota(
        jnp.int32, (PRE, PRE), 1
    )
    masked = jnp.where(causal, prompt_scores, neg_big)
    top_prompt = jnp.max(masked, axis=-1, keepdims=True)
    prompt_weights = jnp.where(causal, jnp.exp(masked - top_prompt), 0.0)
    prompt_num = jnp.einsum(
        "kgqt,tkh->qkgh",
        prompt_weights,
        prompt_v,
        precision=lax.Precision.HIGHEST,
        preferred_element_type=jnp.float32,
    )
    prompt_den = jnp.sum(prompt_weights, axis=-1).transpose(2, 0, 1)
    prompt_out = (prompt_num / prompt_den[..., None]).astype(jnp.bfloat16).reshape(PRE, -1)
    attn = jnp.concatenate([decode_out, prompt_out], axis=0)
    head_terms = jnp.dot(attn, out_proj, preferred_element_type=jnp.float32)
    column_start = mp_index * width_local
    own_columns = lax.dynamic_slice_in_dim(
        head_terms, column_start, width_local, 1
    ) + residual.astype(jnp.float32)
    head_terms = lax.dynamic_update_slice_in_dim(head_terms, own_columns, column_start, 1)
    hidden_full = lax.psum(head_terms, "mp")
    normed = (
        hidden_full
        * lax.rsqrt(jnp.mean(hidden_full * hidden_full, axis=1, keepdims=True) + eps_norm)
        * attn_gain[None, :]
    ).astype(jnp.bfloat16)
    hidden_cols = lax.dynamic_slice_in_dim(hidden_full, column_start, width_local, 1)
    tok_rows = residual.shape[0]
    pairs = routes.reshape(-1)
    onehot = (pairs[:, None] == lax.broadcasted_iota(jnp.int32, (1, E), 1)).astype(jnp.int32)
    slots = jnp.sum((jnp.cumsum(onehot, axis=0) - onehot) * onehot, axis=1)
    target = pairs * C + slots
    cells = lax.broadcasted_iota(jnp.int32, (1, E * C), 1)
    hits = (target[:, None] == cells).reshape(tok_rows, 2, E * C)
    dispatch = jnp.any(hits, axis=1).astype(jnp.bfloat16)
    combine = jnp.sum(jnp.where(hits, route_weight[:, :, None], 0.0), axis=1)
    buffer = lax.dot_general(
        dispatch, normed, (((0,), (0,)), ((), ())), preferred_element_type=jnp.float32
    ).astype(jnp.bfloat16)
    send = jnp.repeat(buffer.reshape(E, C, normed.shape[1]), dp_count // E, axis=0)
    arrived = lax.all_to_all(send, "dp", split_axis=0, concat_axis=0, tiled=True)
    gate_sum = jnp.einsum("scd,df->scf", arrived, gate_proj, preferred_element_type=jnp.float32)
    up_sum = jnp.einsum("scd,df->scf", arrived, up_proj, preferred_element_type=jnp.float32)
    hidden = (jax.nn.silu(gate_sum) * up_sum).astype(jnp.bfloat16)
    down_part = jnp.einsum("scf,fd->scd", hidden, down_proj, preferred_element_type=jnp.float32)
    shares = lax.psum_scatter(
        down_part.astype(jnp.bfloat16), "mp", scatter_dimension=2, tiled=True
    ).astype(jnp.float32)
    returned = lax.all_to_all(shares, "dp", split_axis=0, concat_axis=0, tiled=True)
    back = (
        returned.reshape(E, dp_count // E, C, width_local).sum(axis=1).reshape(E * C, width_local)
    )
    moe_rows = jnp.dot(
        combine, back, precision=lax.Precision.HIGHEST, preferred_element_type=jnp.float32
    )
    mixed = hidden_cols + moe_rows
    square_last = lax.psum(jnp.sum(mixed * mixed, axis=1), "mp")
    scaled = mixed * lax.rsqrt(square_last / D + eps_norm)[:, None] * final_gain[None, :]
    return scaled.astype(jnp.bfloat16)


def solution(mesh):
    return jax.shard_map(
        local,
        mesh=mesh,
        in_specs=(
            P("dp", "mp"),
            P("dp", "mp"),
            P("dp", "mp"),
            P("dp", "mp"),
            P("dp", None, "mp"),
            P("dp", None, "mp"),
            P(),
            P(),
            P("mp", None),
            P(),
            P("dp", None),
            P("dp", None),
            P(None, ("dp", "mp")),
            P(None, ("dp", "mp")),
            P(("dp", "mp"), None),
            P("mp"),
        ),
        out_specs=P("dp", "mp"),
        check_vma=False,
    )
```

profile of v0, /device:TPU:1, one launch (start us, length us, event | category | flops | bytes accessed | tf_op | source)
XLA Modules:
  0.0 385.3 jit_solution(8558500685093032469)
XLA Ops:
  6.5 1.6 fusion.67
  8.2 0.7 fusion.64
  8.9 0.3 reduce-window.15
  9.4 0.8 fusion.63
  10.1 1.0 select_reduce_fusion.1
  11.3 0.9 select_reduce_fusion.3
  12.6 41.5 %all-gather.2.cloned.1.call-done = bf16[1024,512]{1,0:T(8,128)(2,1)} async-done(((bf16[64,512]{1,0:T(8,128)(2,1)}), bf16[1024,512]{1,0:T(8,128)(2,1)}) %all-gather.2.cloned.1.call-update) | async-done | bytes 1048592 | tf_op jit(solution)/shard_map/all_gather | solution.py:97
  54.2 1.3 reshape.430
  55.5 0.7 gather_fusion
  56.3 0.5 fusion.69
  56.8 0.3 select_reduce_fusion
  57.3 0.7 gather_fusion.1
  58.0 0.4 fusion.25
  58.4 0.8 fusion.70
  59.2 0.7 reshape.468
  59.9 5.0 %all-to-all-start.2 = ((f32[16,1,256]{2,1,0:T(1,128)}), f32[16,1,256]{2,1,0:T(1,128)S(1)}, u32[]{:S(2)}, u32[]{:S(2)}) async-start(f32[16,1,256]{2,1,0:T(1,128)} %reshape.468), calls=%async_computation.2 | async-start | bytes 32768 | tf_op jit(solution)/shard_map/all_to_all | solution.py:117
  64.9 0.7 fusion.7
  65.8 0.7 reshape.466
  66.5 4.8 %all-to-all-done.2 = f32[16,1,256]{2,1,0:T(1,128)S(1)} async-done(((f32[16,1,256]{2,1,0:T(1,128)}), f32[16,1,256]{2,1,0:T(1,128)S(1)}, u32[]{:S(2)}, u32[]{:S(2)}) %all-to-all-start.2) | async-done | bytes 16416 | tf_op jit(solution)/shard_map/all_to_all | solution.py:117
  71.3 3.5 all-to-all-start.1
  74.8 2.4 convolution_bitcast_fusion
  77.2 4.0 %all-to-all-done.1 = f32[16,1,256]{2,1,0:T(1,128)S(1)} async-done(((f32[16,1,256]{2,1,0:T(1,128)}), f32[16,1,256]{2,1,0:T(1,128)S(1)}, u32[]{:S(2)}, u32[]{:S(2)}) %all-to-all-start.1) | async-done | bytes 16416 | tf_op jit(solution)/shard_map/all_to_all | solution.py:116
  81.2 3.7 all-to-all-start
  85.6 0.3 fusion.12
  86.0 0.5 broadcast.295
  86.5 0.7 reduce.15
  87.3 0.7 reduce.14
  88.1 21.4 %all-to-all-done = f32[16,64,1,4,128]{4,1,3,2,0:T(8,128)S(1)} async-done(((f32[16,64,1,4,128]{4,1,3,2,0:T(8,128)}), f32[16,64,1,4,128]{4,1,3,2,0:T(8,128)S(1)}, u32[]{:S(2)}, u32[]{:S(2)}) %all-to-all-start) | async-done | bytes 2097184 | tf_op jit(solution)/shard_map/all_to_all | solution.py:118
  109.6 0.7 bitcast_reduce_fusion
  110.4 2.9 fusion.26
  113.5 1.3 copy-done.2
  115.3 0.6 reduce-window.19
  116.5 65.0 %all-reduce.2.cloned.1.call-done = f32[128,4096]{1,0:T(8,128)} async-done(((f32[128,4096]{1,0:T(8,128)}), f32[128,4096]{1,0:T(8,128)}) %all-reduce.2.cloned.1.call-update) | async-done | bytes 2097168 | tf_op jit(solution)/shard_map/psum | solution.py:170
  181.5 2.0 multiply_reduce_fusion
  183.8 1.1 convolution_convert_fusion.1
  184.8 0.8 broadcast_in_dim.146
  185.6 77.8 %all_to_all.25 = bf16[16,48,4096]{2,1,0:T(8,128)(2,1)S(1)} all-to-all(bf16[16,48,4096]{2,1,0:T(8,128)(2,1)S(1)} %bitcast.149), channel_id=1, replica_groups=mesh['dp'=16,'mp'=8] {'dp'}, dimensions={0} | all-to-all | bytes 12582912 | tf_op jit(solution)/shard_map/all_to_all | solution.py:190
  263.4 7.5 %fusion.1 = f32[16,48,768]{2,1,0:T(8,128)S(1)} fusion(bf16[16,48,4096]{2,1,0:T(8,128)(2,1)S(1)} %all_to_all.25, bf16[4096,768]{1,0:T(8,128)(2,1)} %param.29), kind=kOutput, calls=%fused_computation.4 | convolution fusion | flops 4831838208 | bytes 14942208 | tf_op jit(solution)/shard_map/scd,df->scf/dot_general | solution.py:192
  270.9 5.3 %multiply_convert_fusion = bf16[16,48,768]{2,1,0:T(8,128)(2,1)S(1)} fusion(f32[16,48,768]{2,1,0:T(8,128)S(1)} %fusion.1, bf16[16,48,4096]{2,1,0:T(8,128)(2,1)S(1)} %all_to_all.25, bf16[4096,768]{1,0:T(8,128)(2,1)S(1)} %bitcast.157), kind=kOutput, calls=%fused_computation.9 | convolution fusion | flops 4835377152 | bytes 16121856 | tf_op jit(solution)/shard_map/scd,df->scf/dot_general | solution.py:191
  276.3 6.9 %convolution_convert_fusion = bf16[16,48,4096]{2,1,0:T(8,128)(2,1)} fusion(bf16[16,48,768]{2,1,0:T(8,128)(2,1)S(1)} %multiply_convert_fusion, bf16[768,4096]{1,0:T(8,128)(2,1)S(1)} %bitcast.159), kind=kOutput, calls=%fused_computation.2 | convolution fusion | flops 4834983936 | bytes 13762560 | tf_op jit(solution)/shard_map/scf,fd->scd/dot_general | solution.py:194
  283.2 44.1 %reduce-scatter.2.cloned.1.call-done = bf16[16,48,512]{2,1,0:T(8,128)(2,1)} async-done(((bf16[16,48,4096]{2,1,0:T(8,128)(2,1)}), bf16[16,48,512]{2,1,0:T(8,128)(2,1)}) %reduce-scatter.2.cloned.1.call-update) | async-done | bytes 786448 | tf_op jit(solution)/shard_map/reduce_scatter | solution.py:195
  327.3 2.5 convert_element_type.63
  329.8 6.8 %all-to-all-start.4 = ((f32[16,48,512]{2,1,0:T(8,128)}), f32[16,48,512]{2,1,0:T(8,128)}, u32[]{:S(2)}, u32[]{:S(2)}) async-start(f32[16,48,512]{2,1,0:T(8,128)} %convert_element_type.63), calls=%async_computation.5 | async-start | bytes 3145728 | tf_op jit(solution)/shard_map/all_to_all | solution.py:198
  336.7 21.0 %all-to-all-done.4 = f32[16,48,512]{2,1,0:T(8,128)} async-done(((f32[16,48,512]{2,1,0:T(8,128)}), f32[16,48,512]{2,1,0:T(8,128)}, u32[]{:S(2)}, u32[]{:S(2)}) %all-to-all-start.4) | async-done | bytes 1572896 | tf_op jit(solution)/shard_map/all_to_all | solution.py:198
  357.7 1.6 bitcast_reduce_fusion.1
  359.3 0.7 multiply_reduce_fusion.1
  360.1 17.9 %psum.15 = f32[128]{0:T(128)S(1)} all-reduce(f32[128]{0:T(128)S(1)} %get-tuple-element.20), channel_id=1, replica_groups=mesh['dp'=16,'mp'=8] {'mp'}, use_global_device_ids=true, to_apply=%region_24.25 | all-reduce | flops 128 | bytes 1024 | tf_op jit(solution)/shard_map/psum | solution.py:206
  378.0 0.8 multiply_convert_fusion.3
  (93 shorter events, 4.1 us)
Async XLA Ops:
  6.5 58.3 %copy-start = (bf16[128,16,128]{2,1,0:T(8,128)(2,1)S(1)}, bf16[128,16,128]{2,1,0:T(8,128)(2,1)}, u32[]{:S(2)}) copy-start(bf16[128,16,128]{2,1,0:T(8,128)(2,1)} %param.21) | copy-start | bytes 1572868
  6.5 49.7 %copy-start.5 = (bf16[128,16,128]{2,1,0:T(8,128)(2,1)S(1)}, bf16[128,16,128]{2,1,0:T(8,128)(2,1)}, u32[]{:S(2)}) copy-start(bf16[128,16,128]{2,1,0:T(8,128)(2,1)} %param.20) | copy-start | bytes 1572868
  6.5 47.6 %all-gather.2.cloned.1.call-start = ((), (), s32[]{:S(2)}) async-start(), calls=%async_computation.6 | async-start | bytes 1114112 | tf_op jit(solution)/shard_map/all_gather | solution.py:97
  59.9 11.4 %all-to-all-start.2 = ((f32[16,1,256]{2,1,0:T(1,128)}), f32[16,1,256]{2,1,0:T(1,128)S(1)}, u32[]{:S(2)}, u32[]{:S(2)}) async-start(f32[16,1,256]{2,1,0:T(1,128)} %reshape.468), calls=%async_computation.2 | async-start | bytes 32768 | tf_op jit(solution)/shard_map/all_to_all | solution.py:117
  71.3 9.9 %all-to-all-start.1 = ((f32[16,1,256]{2,1,0:T(1,128)}), f32[16,1,256]{2,1,0:T(1,128)S(1)}, u32[]{:S(2)}, u32[]{:S(2)}) async-start(f32[16,1,256]{2,1,0:T(1,128)} %reshape.466), calls=%async_computation.1 | async-start | bytes 32768 | tf_op jit(solution)/shard_map/all_to_all | solution.py:116
  77.2 7.8 %copy-start.4 = (bf16[64,512]{1,0:T(8,128)(2,1)S(1)}, bf16[64,512]{1,0:T(8,128)(2,1)}, u32[]{:S(2)}) copy-start(bf16[64,512]{1,0:T(8,128)(2,1)} %get-tuple-element.12) | copy-start | bytes 196612
  77.2 7.8 %copy-start.7 = (bf16[128,128]{1,0:T(8,128)(2,1)S(1)}, bf16[128,128]{1,0:T(8,128)(2,1)}, u32[]{:S(2)}) copy-start(bf16[128,128]{1,0:T(8,128)(2,1)} %param.18) | copy-start | bytes 98308
  77.2 8.4 %copy-start.9 = (bf16[128,128]{1,0:T(8,128)(2,1)S(1)}, bf16[128,128]{1,0:T(8,128)(2,1)}, u32[]{:S(2)}) copy-start(bf16[128,128]{1,0:T(8,128)(2,1)} %param.19) | copy-start | bytes 98308
  81.2 28.4 %all-to-all-start = ((f32[16,64,1,4,128]{4,1,3,2,0:T(8,128)}), f32[16,64,1,4,128]{4,1,3,2,0:T(8,128)S(1)}, u32[]{:S(2)}, u32[]{:S(2)}) async-start(f32[16,64,1,4,128]{4,1,3,2,0:T(8,128)} %convolution_bitcast_fusion), calls=%async_computation | async-start | bytes 4194304 | tf_op jit(solution)/shard_map/all_to_all | solution.py:118
  84.9 96.6 %all-reduce.2.cloned.1.call-start = ((), (), s32[]{:S(2)}) async-start(), calls=%async_computation.7 | async-start | bytes 4194304 | tf_op jit(solution)/shard_map/psum | solution.py:170
  110.4 3.0 copy-start.6
  113.4 1.4 copy-start.10
  113.5 1.3 copy-start.2
  113.5 70.0 %copy-start.8 = (f32[4096]{0:T(1024)S(1)}, f32[4096]{0:T(1024)}, u32[]{:S(2)}) copy-start(f32[4096]{0:T(1024)} %param.25) | copy-start | bytes 49156
  114.8 212.5 %reduce-scatter.2.cloned.1.call-start = ((), (), s32[]{:S(2)}) async-start(), calls=%async_computation.8 | async-start | bytes 7077888 | tf_op jit(solution)/shard_map/reduce_scatter | solution.py:195
  181.5 2.2 copy-start.3
  185.6 85.3 %slice-start = ((s8[6291456]{0:T(1024)(128)(4,1)}), s8[4194304]{0:T(1024)(128)(4,1)S(1)}, s32[]{:S(2)}) async-start(s8[6291456]{0:T(1024)(128)(4,1)} %bitcast.156), calls=%async_computation.9 | async-start | bytes 8388608
  263.4 7.5 %slice-start.1 = ((s8[6291456]{0:T(1024)(128)(4,1)}), s8[2097152]{0:T(1024)(128)(4,1)S(1)}, s32[]{:S(2)}) async-start(s8[6291456]{0:T(1024)(128)(4,1)} %bitcast.156), calls=%async_computation.10 | async-start | bytes 4194304
  263.4 12.8 %slice-start.2 = ((s8[6291456]{0:T(1024)(128)(4,1)}), s8[4194304]{0:T(1024)(128)(4,1)S(1)}, s32[]{:S(2)}) async-start(s8[6291456]{0:T(1024)(128)(4,1)} %bitcast.158), calls=%async_computation.11 | async-start | bytes 8388608
  270.9 5.3 %slice-start.3 = ((s8[6291456]{0:T(1024)(128)(4,1)}), s8[2097152]{0:T(1024)(128)(4,1)S(1)}, s32[]{:S(2)}) async-start(s8[6291456]{0:T(1024)(128)(4,1)} %bitcast.158), calls=%async_computation.12 | async-start | bytes 4194304
  283.2 53.4 %copy-start.12 = (f32[128,2]{0,1:T(2,128)S(1)}, f32[128,2]{0,1:T(2,128)}, u32[]{:S(2)}) copy-start(f32[128,2]{0,1:T(2,128)} %param.27) | copy-start | bytes 3076
  329.8 27.9 %all-to-all-start.4 = ((f32[16,48,512]{2,1,0:T(8,128)}), f32[16,48,512]{2,1,0:T(8,128)}, u32[]{:S(2)}, u32[]{:S(2)}) async-start(f32[16,48,512]{2,1,0:T(8,128)} %convert_element_type.63), calls=%async_computation.5 | async-start | bytes 3145728 | tf_op jit(solution)/shard_map/all_to_all | solution.py:198
  336.6 41.4 %copy-start.11 = (f32[512]{0:T(512)S(1)}, f32[512]{0:T(512)}, u32[]{:S(2)}) copy-start(f32[512]{0:T(512)} %param.31) | copy-start | bytes 6148
  336.6 42.2 %copy-start.1 = (bf16[128,16,128]{2,1,0:T(8,128)(2,1)S(1)}, bf16[128,16,128]{2,1,0:T(8,128)(2,1)}, u32[]{:S(2)}) copy-start(bf16[128,16,128]{2,1,0:T(8,128)(2,1)} %param.21) | copy-start | bytes 1572868
Sparse Core Ops, SparseCore 0:
  9.5 44.6 all-gather.1
  114.9 66.5 all-reduce.1
  283.3 43.9 reduce-scatter.1
where the time goes:
time: 387 us; the launch traced here: 385 us
  waiting for transfers between devices  202 us (52%)
  blocking collectives  95.7 us (25%)
  matrix products  29.4 us (8%)
  starting transfers between devices  19 us (5%)
  other arithmetic  15.1 us (4%)
  between operations  13.7 us (4%)
  local copies, waits for them, and re-layouts  10.6 us (3%)
    all_to_all x1, blocking collectives, local(): lax.all_to_all(send, 'dp', split_axis=0, concat_axis=0, tiled=True)  77.8 us
    psum x1, waiting for transfers between devices, local(): hidden_full = lax.psum(head_terms, 'mp')  65 us
    reduce_scatter x1, waiting for transfers between devices, local(): lax.psum_scatter(down_part.astype(jnp.bfloat16), 'mp', scatter_dimension=...  44.1 us
    all_gather x1, waiting for transfers between devices, local(): gathered = lax.all_gather(queries[:DEC], 'dp', axis=0, tiled=True)  41.5 us
    all_to_all x1, waiting for transfers between devices, local(): lax.all_to_all(weighted, 'dp', split_axis=0, concat_axis=0, tiled=True)  21.4 us
    all_to_all x1, waiting for transfers between devices, local(): lax.all_to_all(shares, 'dp', split_axis=0, concat_axis=0, tiled=True)  21 us
    psum x1, blocking collectives, local(): square_last = lax.psum(jnp.sum(mixed * mixed, axis=1), 'mp')  17.9 us
  transfers between devices with their start and end apart: 7, of which 7 were waited for; matrix products, arithmetic and copies ran while one was open for 3% of the time, Pallas kernels for 0%

commit v1 on v0

--- a/solution.py
+++ b/solution.py
@@ -1,6 +1,10 @@
+import functools
+
 import jax
 import jax.numpy as jnp
 from jax import lax
+from jax.experimental import pallas as pl
+from jax.experimental.pallas import tpu as pltpu
 from jax.sharding import PartitionSpec as P
 
 D = 4096
@@ -12,10 +16,520 @@
 DEC = 64
 PRE = 64
 C = 48
-
+NDP = 16
+NCH = 3
+SL = C // NCH
+RC = NDP * SL
+FW = 512
+HID = 768
+
+MESH = pl.DeviceIdType.MESH
+DMA = pltpu.SemaphoreType.DMA
+BF = jnp.bfloat16
+F32 = jnp.float32
 
 neg_big = -1e30
 eps_norm = 1e-05
+
+
+def remote(src, dst, send_sem, recv_sem, device):
+    return pltpu.make_async_remote_copy(
+        src_ref=src,
+        dst_ref=dst,
+        send_sem=send_sem,
+        recv_sem=recv_sem,
+        device_id=device,
+        device_id_type=MESH,
+    )
+
+
+def greet(devices):
+    barrier = pltpu.get_barrier_semaphore()
+    for device in devices:
+        pl.semaphore_signal(barrier, inc=1, device_id=device, device_id_type=MESH)
+    pl.semaphore_wait(barrier, len(devices))
+
+
+def comm_params(collective_id):
+    return pltpu.CompilerParams(
+        collective_id=collective_id, has_side_effects=True, vmem_limit_bytes=60 << 20
+    )
+
+
+def vmem(count):
+    return [pl.BlockSpec(memory_space=pltpu.VMEM)] * count
+
+
+def gather_kernel(src, dst, send, recv, own_sem):
+    me = lax.axis_index("dp")
+    peers = [lax.rem(me + k, NDP) for k in range(1, NDP)]
+    greet([{"dp": p} for p in peers])
+    own = pltpu.make_async_copy(src, dst.at[me], own_sem)
+    own.start()
+    copies = []
+    for k, p in enumerate(peers):
+        copies.append(remote(src, dst.at[me], send.at[k], recv.at[k], {"dp": p}))
+        copies[-1].start()
+    for copy in copies:
+        copy.wait()
+    own.wait()
+
+
+def gather_dp(x, collective_id):
+    return pl.pallas_call(
+        gather_kernel,
+        out_shape=jax.ShapeDtypeStruct((NDP,) + x.shape, x.dtype),
+        in_specs=vmem(1),
+        out_specs=vmem(1)[0],
+        scratch_shapes=[DMA((NDP - 1,)), DMA((NDP - 1,)), DMA],
+        compiler_params=comm_params(collective_id),
+        name="gather_queries",
+    )(x)
+
+
+def swap_kernel(values, stats, values_out, stats_out, send, recv, own_sems):
+    me = lax.axis_index("dp")
+    peers = [lax.rem(me + k, NDP) for k in range(1, NDP)]
+    greet([{"dp": p} for p in peers])
+    own = [
+        pltpu.make_async_copy(values.at[me], values_out.at[me], own_sems.at[0]),
+        pltpu.make_async_copy(stats.at[me], stats_out.at[me], own_sems.at[1]),
+    ]
+    for copy in own:
+        copy.start()
+    copies = []
+    for k, p in enumerate(peers):
+        copies.append(
+            remote(stats.at[p], stats_out.at[me], send.at[1, k], recv.at[1, k], {"dp": p})
+        )
+        copies.append(
+            remote(values.at[p], values_out.at[me], send.at[0, k], recv.at[0, k], {"dp": p})
+        )
+    for copy in copies:
+        copy.start()
+    for copy in copies:
+        copy.wait()
+    for copy in own:
+        copy.wait()
+
+
+def swap_partials(values, stats, collective_id):
+    return pl.pallas_call(
+        swap_kernel,
+        out_shape=(
+            jax.ShapeDtypeStruct(values.shape, values.dtype),
+            jax.ShapeDtypeStruct(stats.shape, stats.dtype),
+        ),
+        in_specs=vmem(2),
+        out_specs=tuple(vmem(2)),
+        scratch_shapes=[DMA((2, NDP - 1)), DMA((2, NDP - 1)), DMA((2,))],
+        compiler_params=comm_params(collective_id),
+        name="swap_partials",
+    )(values, stats)
+
+
+def hidden_kernel(parts, residual, gain, hidden, normed, got, squares, send, recv, send2, recv2):
+    me = lax.axis_index("mp")
+    peers = [lax.rem(me + k, 8) for k in range(1, 8)]
+    greet([{"mp": p} for p in peers])
+    copies = []
+    for k, p in enumerate(peers):
+        copies.append(remote(parts.at[p], got.at[k], send.at[k], recv.at[k], {"mp": p}))
+        copies[-1].start()
+    total = residual[...].astype(F32) + parts[me].astype(F32)
+    for k, copy in enumerate(copies):
+        copy.wait_recv()
+        total = total + got[k].astype(F32)
+    hidden[...] = total
+    squares[7] = jnp.broadcast_to(jnp.sum(total * total, axis=1, keepdims=True), (128, 128))
+    copies2 = []
+    for k, p in enumerate(peers):
+        copies2.append(remote(squares.at[7], squares.at[k], send2.at[k], recv2.at[k], {"mp": p}))
+        copies2[-1].start()
+    for copy in copies2:
+        copy.wait_recv()
+    summed = squares[0]
+    for k in range(1, 8):
+        summed = summed + squares[k]
+    scale = lax.rsqrt(summed[:, :1] / D + eps_norm)
+    normed[...] = (hidden[...] * scale * gain[...]).astype(BF)
+    for copy in copies + copies2:
+        copy.wait_send()
+
+
+def hidden_and_norm(parts, residual, gain, collective_id):
+    rows = residual.shape[0]
+    return pl.pallas_call(
+        hidden_kernel,
+        out_shape=(
+            jax.ShapeDtypeStruct((rows, FW), F32),
+            jax.ShapeDtypeStruct((rows, FW), BF),
+        ),
+        in_specs=vmem(3),
+        out_specs=tuple(vmem(2)),
+        scratch_shapes=[
+            pltpu.VMEM((7, rows, FW), BF),
+            pltpu.VMEM((8, rows, 128), F32),
+            DMA((7,)),
+            DMA((7,)),
+            DMA((7,)),
+            DMA((7,)),
+        ],
+        compiler_params=comm_params(collective_id),
+        name="hidden_and_norm",
+    )(parts, residual, gain)
+
+
+def experts_kernel(
+    send,
+    wg,
+    wu,
+    wd,
+    ret,
+    x_all,
+    wg_v,
+    wu_v,
+    wd_v,
+    hid,
+    part,
+    own_part,
+    hop_in,
+    hop_out,
+    fin,
+    out,
+    w_sems,
+    wp_send,
+    wp_recv,
+    a_send,
+    a_recv,
+    a_own,
+    g_send,
+    g_recv,
+    f_send,
+    f_recv,
+    p_send,
+    p_recv,
+    h_send,
+    h_recv,
+    t_send,
+    t_recv,
+    n_send,
+    n_recv,
+    r_send,
+    r_recv,
+    r_own,
+):
+    dp = lax.axis_index("dp")
+    mp = lax.axis_index("mp")
+    x, c = mp // 2, lax.rem(mp, 2)
+    xr, xo, xl = lax.rem(x + 1, 4), lax.rem(x + 2, 4), lax.rem(x + 3, 4)
+    mr, mo, ml = xr * 2 + c, xo * 2 + c, xl * 2 + c
+    right, left, mate = {"mp": mr}, {"mp": ml}, {"mp": x * 2 + 1 - c}
+    sides = (right, left)
+    peers = [lax.rem(dp + k, NDP) for k in range(1, NDP)]
+    half = RC // 2
+
+    w_copies = [
+        pltpu.make_async_copy(wg, wg_v, w_sems.at[0]),
+        pltpu.make_async_copy(wu, wu_v, w_sems.at[1]),
+    ]
+    for j in range(4):
+        w_copies.append(
+            pltpu.make_async_copy(
+                wd.at[:, pl.ds(pl.multiple_of(j * 1024 + c * FW, FW), FW)],
+                wd_v.at[0, :, pl.ds(j * FW, FW)],
+                w_sems.at[2 + j],
+            )
+        )
+    greet([{"dp": p} for p in peers] + [right, left, mate])
+
+    def columns(owner):
+        return pl.ds(pl.multiple_of(owner * FW, FW), FW)
+
+    sent = []
+
+    def go(copy):
+        copy.start()
+        sent.append(copy)
+
+    out_copies, own_copies = [], []
+    for ch in range(NCH):
+        rows = pl.ds(pl.multiple_of(dp * SL, SL), SL)
+        own = pltpu.make_async_copy(send.at[ch, dp], x_all.at[ch, rows, columns(mp)], a_own.at[ch])
+        own.start()
+        own_copies.append(own)
+        cs = []
+        for k, p in enumerate(peers):
+            copy = remote(
+                send.at[ch, p],
+                x_all.at[ch, rows, columns(mp)],
+                a_send.at[ch, k],
+                a_recv.at[ch, k],
+                {"dp": p},
+            )
+            go(copy)
+            cs.append(copy)
+        out_copies.append(cs)
+    for copy in w_copies:
+        copy.start()
+    mate_w = []
+    for j in range(4):
+        mate_w.append(
+            remote(
+                wd.at[:, pl.ds(pl.multiple_of(j * 1024 + (1 - c) * FW, FW), FW)],
+                wd_v.at[1, :, pl.ds(j * FW, FW)],
+                wp_send.at[j],
+                wp_recv.at[j],
+                mate,
+            )
+        )
+        go(mate_w[j])
+
+    def block(ch, h, owner):
+        return x_all.at[ch, pl.ds(h * half, half), columns(owner)]
+
+    def whole(ch, owner):
+        return x_all.at[ch, :, columns(owner)]
+
+    def neighbour(ch, side, h):
+        return remote(block(ch, h, mp), block(ch, h, mp), g_send.at[ch, side, h], g_recv.at[ch, side, h], sides[side])
+
+    def onward(ch, side):
+        owner = (ml, mr)[side]
+        return remote(
+            block(ch, side, owner), block(ch, side, owner), f_send.at[ch, side], f_recv.at[ch, side], sides[side]
+        )
+
+    def to_mate(ch, which):
+        owner = (mp, ml, mr, mo)[which]
+        return remote(whole(ch, owner), whole(ch, owner), p_send.at[ch, which], p_recv.at[ch, which], mate)
+
+    def spread_own(ch):
+        for copy in out_copies[ch]:
+            copy.wait_recv()
+        own_copies[ch].wait()
+        for h in range(2):
+            go(neighbour(ch, 0, h))
+            go(neighbour(ch, 1, 1 - h))
+        go(to_mate(ch, 0))
+
+    def spread_on(ch):
+        for side in range(2):
+            neighbour(ch, side, side).wait_recv()
+            go(onward(ch, side))
+
+    def spread_rest(ch):
+        for side in range(2):
+            neighbour(ch, side, 1 - side).wait_recv()
+            go(to_mate(ch, 1 + side))
+
+    def spread_far(ch):
+        for side in range(2):
+            onward(ch, side).wait_recv()
+        go(to_mate(ch, 3))
+
+    def spread_end(ch):
+        for which in range(4):
+            to_mate(ch, which).wait_recv()
+
+    def hidden_send(ch):
+        return remote(hid.at[ch, 0], hid.at[ch, 1], h_send.at[ch], h_recv.at[ch], mate)
+
+    def gate_up(ch, n):
+        cols = pl.ds(n * 256, 256)
+        rows = x_all[ch]
+        g = jnp.dot(rows, wg_v[:, cols], preferred_element_type=F32)
+        u = jnp.dot(rows, wu_v[:, cols], preferred_element_type=F32)
+        hid[ch, 0, :, cols] = (g / (1.0 + jnp.exp(-g)) * u).astype(BF)
+
+    def down(ch, owner):
+        cols = columns(owner)
+        return jnp.dot(hid[ch, 0], wd_v[0, :, cols], preferred_element_type=F32) + jnp.dot(
+            hid[ch, 1], wd_v[1, :, cols], preferred_element_type=F32
+        )
+
+    def rows_of(h):
+        return pl.ds(h * half, half)
+
+    def hop(ch, side):
+        return remote(
+            part.at[ch, 0, rows_of(side)], hop_in.at[ch, side], t_send.at[ch, side], t_recv.at[ch, side], sides[side]
+        )
+
+    def near(ch, side, h, src):
+        return remote(src, fin.at[ch, side, rows_of(h)], n_send.at[ch, side, h], n_recv.at[ch, side, h], sides[side])
+
+    def reduce_start(ch):
+        part[ch, 0] = down(ch, xo).astype(BF)
+        for side in range(2):
+            go(hop(ch, side))
+        for side in range(2):
+            part[ch, 1 + side] = down(ch, (xr, xl)[side]).astype(BF)
+            go(near(ch, side, 1 - side, part.at[ch, 1 + side, rows_of(1 - side)]))
+
+    def reduce_own(ch):
+        own_part[ch] = down(ch, x)
+
+    def reduce_hop(ch):
+        for side in range(2):
+            hop(ch, side).wait_recv()
+            hop_out[ch, side] = (
+                part[ch, 1 + side, rows_of(side), :].astype(F32) + hop_in[ch, side].astype(F32)
+            ).astype(BF)
+            go(near(ch, side, side, hop_out.at[ch, side]))
+
+    ret_copies = []
+
+    def reduce_end(ch):
+        for side in range(2):
+            for h in range(2):
+                near(ch, side, h, hop_out.at[ch, side]).wait_recv()
+        total = own_part[ch] + fin[ch, 0].astype(F32) + fin[ch, 1].astype(F32)
+        out[ch] = total.astype(BF)
+        own = pltpu.make_async_copy(
+            out.at[ch, pl.ds(pl.multiple_of(dp * SL, SL), SL)], ret.at[ch, dp], r_own.at[ch]
+        )
+        own.start()
+        cs = [own]
+        for k, p in enumerate(peers):
+            copy = remote(
+                out.at[ch, pl.ds(pl.multiple_of(p * SL, SL), SL)],
+                ret.at[ch, dp],
+                r_send.at[ch, k],
+                r_recv.at[ch, k],
+                {"dp": p},
+            )
+            copy.start()
+            cs.append(copy)
+        ret_copies.extend(cs)
+
+    spread_own(0)
+    spread_on(0)
+    spread_own(1)
+    spread_rest(0)
+    spread_far(0)
+    for copy in w_copies[:2]:
+        copy.wait()
+    spread_on(1)
+    spread_own(2)
+    spread_end(0)
+    for ch in range(NCH):
+        gate_up(ch, 0)
+        if ch == 0:
+            spread_rest(1)
+        if ch == 1:
+            reduce_hop(0)
+        if ch == 2:
+            reduce_hop(1)
+        gate_up(ch, 1)
+        if ch == 0:
+            spread_far(1)
+        if ch == 1:
+            spread_rest(2)
+        gate_up(ch, 2)
+        go(hidden_send(ch))
+        if ch == 0:
+            spread_on(2)
+            for copy in w_copies[2:]:
+                copy.wait()
+            for copy in mate_w:
+                copy.wait_recv()
+        if ch == 1:
+            spread_far(2)
+            reduce_end(0)
+        if ch == 2:
+            reduce_end(1)
+        hidden_send(ch).wait_recv()
+        reduce_start(ch)
+        reduce_own(ch)
+        if ch < 2:
+            spread_end(ch + 1)
+    reduce_hop(2)
+    reduce_end(2)
+    for copy in ret_copies:
+        copy.wait()
+    for copy in sent:
+        copy.wait_send()
+
+
+def experts(send, wg, wu, wd, collective_id):
+    anyspace = pl.BlockSpec(memory_space=pl.ANY)
+    return pl.pallas_call(
+        experts_kernel,
+        out_shape=jax.ShapeDtypeStruct((NCH, NDP, SL, FW), BF),
+        in_specs=vmem(1) + [anyspace] * 3,
+        out_specs=vmem(1)[0],
+        scratch_shapes=[
+            pltpu.VMEM((NCH, RC, D), BF),
+            pltpu.VMEM((D, HID), BF),
+            pltpu.VMEM((D, HID), BF),
+            pltpu.VMEM((2, HID, D // 2), BF),
+            pltpu.VMEM((NCH, 2, RC, HID), BF),
+            pltpu.VMEM((NCH, 3, RC, FW), BF),
+            pltpu.VMEM((NCH, RC, FW), F32),
+            pltpu.VMEM((NCH, 2, RC // 2, FW), BF),
+            pltpu.VMEM((NCH, 2, RC // 2, FW), BF),
+            pltpu.VMEM((NCH, 2, RC, FW), BF),
+            pltpu.VMEM((NCH, RC, FW), BF),
+            DMA((6,)),
+            DMA((4,)),
+            DMA((4,)),
+            DMA((NCH, NDP - 1)),
+            DMA((NCH, NDP - 1)),
+            DMA((NCH,)),
+            DMA((NCH, 2, 2)),
+            DMA((NCH, 2, 2)),
+            DMA((NCH, 2)),
+            DMA((NCH, 2)),
+            DMA((NCH, 4)),
+            DMA((NCH, 4)),
+            DMA((NCH,)),
+            DMA((NCH,)),
+            DMA((NCH, 2)),
+            DMA((NCH, 2)),
+            DMA((NCH, 2, 2)),
+            DMA((NCH, 2, 2)),
+            DMA((NCH, NDP - 1)),
+            DMA((NCH, NDP - 1)),
+            DMA((NCH,)),
+        ],
+        compiler_params=comm_params(collective_id),
+        name="experts",
+    )(send, wg, wu, wd)
+
+
+def closing_kernel(mixed, gain, out, squares, send, recv):
+    me = lax.axis_index("mp")
+    peers = [lax.rem(me + k, 8) for k in range(1, 8)]
+    greet([{"mp": p} for p in peers])
+    rows = mixed[...]
+    squares[7] = jnp.broadcast_to(jnp.sum(rows * rows, axis=1, keepdims=True), (128, 128))
+    copies = []
+    for k, p in enumerate(peers):
+        copies.append(remote(squares.at[7], squares.at[k], send.at[k], recv.at[k], {"mp": p}))
+        copies[-1].start()
+    for copy in copies:
+        copy.wait_recv()
+    summed = squares[0]
+    for k in range(1, 8):
+        summed = summed + squares[k]
+    scale = lax.rsqrt(summed[:, :1] / D + eps_norm)
+    out[...] = (mixed[...] * scale * gain[...]).astype(BF)
+    for copy in copies:
+        copy.wait_send()
+
+
+def closing_norm(mixed, gain, collective_id):
+    rows = mixed.shape[0]
+    return pl.pallas_call(
+        closing_kernel,
+        out_shape=jax.ShapeDtypeStruct((rows, FW), BF),
+        in_specs=vmem(2),
+        out_specs=vmem(1)[0],
+        scratch_shapes=[pltpu.VMEM((8, rows, 128), F32), DMA((7,)), DMA((7,))],
+        compiler_params=comm_params(collective_id),
+        name="closing_norm",
+    )(mixed, gain)
 
 
 def page_owner(page_ids, page_order, cache_len):
@@ -94,7 +608,7 @@
     pool_local = cache_keys.shape[0]
     request_total = cache_len.shape[0]
     query_heads = queries[:DEC].reshape(DEC, kv_local, group_size, HD)
-    gathered = lax.all_gather(queries[:DEC], "dp", axis=0, tiled=True)
+    gathered = gather_dp(queries[:DEC], 0)
     gathered_heads = gathered.reshape(request_total, kv_local, group_size, HD)
     page_ids = dp_index * pool_local + lax.broadcasted_iota(jnp.int32, (pool_local,), 0)
     owners, key_ok = page_owner(page_ids, page_order, cache_len)
@@ -109,14 +623,16 @@
         :, None
     ]
     maxima, totals, weighted = fold_pages(maxima, totals, weighted, owned, local_owner)
-    maxima = maxima.reshape(dp_count, DEC, kv_local, group_size)
-    totals = totals.reshape(dp_count, DEC, kv_local, group_size)
-    weighted = weighted.reshape(dp_count, DEC, kv_local, group_size, HD)
-    maxima, totals, weighted = (
-        lax.all_to_all(maxima, "dp", split_axis=0, concat_axis=0, tiled=True),
-        lax.all_to_all(totals, "dp", split_axis=0, concat_axis=0, tiled=True),
-        lax.all_to_all(weighted, "dp", split_axis=0, concat_axis=0, tiled=True),
-    )
+    stats = jnp.concatenate([maxima.reshape(request_total, 4), totals.reshape(request_total, 4)], axis=1)
+    stats = stats.reshape(dp_count, DEC, 8).transpose(0, 2, 1)
+    stats = jnp.pad(stats, ((0, 0), (0, 0), (0, 128 - DEC)))
+    values_in, stats_in = swap_partials(
+        weighted.reshape(dp_count, DEC, FW).astype(BF), stats, 1
+    )
+    stats_in = stats_in[:, :, :DEC].transpose(0, 2, 1)
+    maxima = stats_in[:, :, :4].reshape(dp_count, DEC, kv_local, group_size)
+    totals = stats_in[:, :, 4:].reshape(dp_count, DEC, kv_local, group_size)
+    weighted = values_in.reshape(dp_count, DEC, kv_local, group_size, HD).astype(F32)
     top_cache = jnp.max(maxima, axis=0)
     factors = jnp.exp(maxima - top_cache[None])
     cache_state = (
@@ -161,24 +677,17 @@
     prompt_den = jnp.sum(prompt_weights, axis=-1).transpose(2, 0, 1)
     prompt_out = (prompt_num / prompt_den[..., None]).astype(jnp.bfloat16).reshape(PRE, -1)
     attn = jnp.concatenate([decode_out, prompt_out], axis=0)
-    head_terms = jnp.dot(attn, out_proj, preferred_element_type=jnp.float32)
+    parts = jnp.einsum(
+        "th,hpc->ptc", attn, out_proj.reshape(FW, 8, FW), preferred_element_type=jnp.float32
+    ).astype(BF)
     column_start = mp_index * width_local
-    own_columns = lax.dynamic_slice_in_dim(
-        head_terms, column_start, width_local, 1
-    ) + residual.astype(jnp.float32)
-    head_terms = lax.dynamic_update_slice_in_dim(head_terms, own_columns, column_start, 1)
-    hidden_full = lax.psum(head_terms, "mp")
-    normed = (
-        hidden_full
-        * lax.rsqrt(jnp.mean(hidden_full * hidden_full, axis=1, keepdims=True) + eps_norm)
-        * attn_gain[None, :]
-    ).astype(jnp.bfloat16)
-    hidden_cols = lax.dynamic_slice_in_dim(hidden_full, column_start, width_local, 1)
+    gain_cols = lax.dynamic_slice_in_dim(attn_gain, column_start, width_local, 0)
+    hidden_cols, normed = hidden_and_norm(parts, residual, gain_cols[None, :], 2)
     tok_rows = residual.shape[0]
     pairs = routes.reshape(-1)
     onehot = (pairs[:, None] == lax.broadcasted_iota(jnp.int32, (1, E), 1)).astype(jnp.int32)
     slots = jnp.sum((jnp.cumsum(onehot, axis=0) - onehot) * onehot, axis=1)
-    target = pairs * C + slots
+    target = (slots // SL) * (E * SL) + pairs * SL + slots % SL
     cells = lax.broadcasted_iota(jnp.int32, (1, E * C), 1)
     hits = (target[:, None] == cells).reshape(tok_rows, 2, E * C)
     dispatch = jnp.any(hits, axis=1).astype(jnp.bfloat16)
@@ -186,26 +695,19 @@
     buffer = lax.dot_general(
         dispatch, normed, (((0,), (0,)), ((), ())), preferred_element_type=jnp.float32
     ).astype(jnp.bfloat16)
-    send = jnp.repeat(buffer.reshape(E, C, normed.shape[1]), dp_count // E, axis=0)
-    arrived = lax.all_to_all(send, "dp", split_axis=0, concat_axis=0, tiled=True)
-    gate_sum = jnp.einsum("scd,df->scf", arrived, gate_proj, preferred_element_type=jnp.float32)
-    up_sum = jnp.einsum("scd,df->scf", arrived, up_proj, preferred_element_type=jnp.float32)
-    hidden = (jax.nn.silu(gate_sum) * up_sum).astype(jnp.bfloat16)
-    down_part = jnp.einsum("scf,fd->scd", hidden, down_proj, preferred_element_type=jnp.float32)
-    shares = lax.psum_scatter(
-        down_part.astype(jnp.bfloat16), "mp", scatter_dimension=2, tiled=True
-    ).astype(jnp.float32)
-    returned = lax.all_to_all(shares, "dp", split_axis=0, concat_axis=0, tiled=True)
+    send = jnp.repeat(buffer.reshape(NCH, E, SL, width_local), dp_count // E, axis=1)
+    returned = experts(send, gate_proj, up_proj, down_proj, 3)
     back = (
-        returned.reshape(E, dp_count // E, C, width_local).sum(axis=1).reshape(E * C, width_local)
+        returned.astype(F32)
+        .reshape(NCH, E, dp_count // E, SL, width_local)
+        .sum(axis=2)
+        .reshape(E * C, width_local)
     )
     moe_rows = jnp.dot(
         combine, back, precision=lax.Precision.HIGHEST, preferred_element_type=jnp.float32
     )
     mixed = hidden_cols + moe_rows
-    square_last = lax.psum(jnp.sum(mixed * mixed, axis=1), "mp")
-    scaled = mixed * lax.rsqrt(square_last / D + eps_norm)[:, None] * final_gain[None, :]
-    return scaled.astype(jnp.bfloat16)
+    return closing_norm(mixed, final_gain[None, :], 4)
 
 
 def solution(mesh):

time: 387 us -> 200 us (0.52)
  waiting for transfers between devices: 202 us -> 0 us
  Pallas kernels: 0 us -> 163 us
  blocking collectives: 95.7 us -> 0 us
  starting transfers between devices: 19 us -> 0 us
  matrix products: 29.4 us -> 11.1 us
  between operations: 13.7 us -> 0.42 us
  other arithmetic: 15.1 us -> 9.8 us
  local copies, waits for them, and re-layouts: 10.6 us -> 15.4 us
    pallas_call x0 -> x5, Pallas kernels: none -> 163 us  [the longest x1 77.2 us: experts(): pl.pallas_call(experts_kernel, out_shape=jax.ShapeDtypeStruct((NCH, NDP,...]
    all_to_all x1 -> x0, blocking collectives: 77.8 us -> none  [local(): lax.all_to_all(send, 'dp', split_axis=0, concat_axis=0, tiled=True)]
    psum x1 -> x0, waiting for transfers between devices: 65 us -> none  [local(): hidden_full = lax.psum(head_terms, 'mp')]
    all_to_all x4 -> x0, waiting for transfers between devices: 51.1 us -> none  [the longest x1 21.4 us: local(): lax.all_to_all(weighted, 'dp', split_axis=0, concat_axis=0, tiled=True)]
    reduce_scatter x1 -> x0, waiting for transfers between devices: 44.1 us -> none  [local(): lax.psum_scatter(down_part.astype(jnp.bfloat16), 'mp', scatter_dimension=...]
    all_gather x1 -> x0, waiting for transfers between devices: 41.5 us -> none  [local(): gathered = lax.all_gather(queries[:DEC], 'dp', axis=0, tiled=True)]
    all_to_all x4 -> x0, starting transfers between devices: 18.9 us -> none  [the longest x1 6.76 us: local(): lax.all_to_all(shares, 'dp', split_axis=0, concat_axis=0, tiled=True)]
    dot_general x4 -> x1, matrix products: 22.6 us -> 3.9 us  [local(): jnp.einsum('th,hpc->ptc', attn, out_proj.reshape(FW, 8, FW), preferred_el...]
  transfers between devices with their start and end apart: 7 -> 0, of which waited for: 7 -> 0; matrix products, arithmetic and copies ran while one was open for 3% -> 0% of each run, Pallas kernels for 0% -> 0%
where the time goes in v1:
time: 200 us; the launch traced here: 199 us
  Pallas kernels  163 us (82%)
  local copies, waits for them, and re-layouts  15.4 us (8%)
  matrix products  11.1 us (6%)
  other arithmetic  9.8 us (5%)
    pallas_call x1, Pallas kernels, experts(): pl.pallas_call(experts_kernel, out_shape=jax.ShapeDtypeStruct((NCH, NDP,...  77.2 us
    pallas_call x1, Pallas kernels, hidden_and_norm(): pl.pallas_call(hidden_kernel, out_shape=(jax.ShapeDtypeStruct((rows, FW),...  26 us
    pallas_call x1, Pallas kernels, gather_dp(): pl.pallas_call(gather_kernel, out_shape=jax.ShapeDtypeStruct((NDP,) + x.s...  22.5 us
    pallas_call x1, Pallas kernels, swap_partials(): pl.pallas_call(swap_kernel, out_shape=(jax.ShapeDtypeStruct(values.shape,...  22.3 us
    pallas_call x1, Pallas kernels, closing_norm(): pl.pallas_call(closing_kernel, out_shape=jax.ShapeDtypeStruct((rows, FW),...  14.6 us

profile of v1, /device:TPU:1, one launch (start us, length us, event | category | flops | bytes accessed | tf_op | source)
XLA Modules:
  0.0 199.3 jit_solution(13574742920109898860)
XLA Ops:
  0.0 0.8 fusion.62
  0.8 0.3 reduce-window.15
  1.3 0.8 fusion.61
  2.1 1.0 select_reduce_fusion.1
  3.0 0.2 convert_reduce_fusion.1
  3.2 0.9 select_reduce_fusion.3
  4.4 1.5 fusion.65
  5.9 22.5 %gather_queries.1 = bf16[16,64,512]{2,1,0:T(8,128)(2,1)} custom-call(bf16[64,512]{1,0:T(8,128)(2,1)} %get-tuple-element.22.src), custom_call_target="tpu_custom_call" | custom-call | tf_op jit(solution)/shard_map/gather_queries/pallas_call | solution.py:79
  28.3 1.3 reshape.490
  29.7 0.7 gather_fusion
  30.5 0.5 fusion.67
  30.9 0.4 fusion.24
  31.4 0.2 fusion.15
  31.6 0.3 select_reduce_fusion
  31.8 0.2 copy.68
  32.1 0.6 gather_fusion.1
  32.7 0.8 fusion.16
  33.7 0.6 pad.4.stats
  34.3 0.7 fusion.9
  35.0 0.1 copy.91
  35.2 2.0 %convolution_convert_fusion.values = bf16[16,64,512]{2,1,0:T(8,128)(2,1)} fusion(f32[512,128,1]{1,0,2:T(8,128)S(1)} %bitcast.138, s32[16,64]{1,0:T(8,128)S(1)} %multiply_add_fusion, s32[128]{0:T(128)S(1)} %broadcast_minimum_fusion, pred[128]{0:T(512)(128)(4,1)S(1)} %broadcast_compare_fusion), kind=kOutput, calls=%fused_computation.9 | convolution fusion | flops 806092800 | bytes 1315456 | tf_op jit(solution)/shard_map/pr,pkgh->rkgh/dot_general | solution.py:577
  37.2 22.3 %swap_partials.1 = (bf16[16,64,512]{2,1,0:T(8,128)(2,1)}, f32[16,8,128]{2,1,0:T(8,128)}) custom-call(bf16[16,64,512]{2,1,0:T(8,128)(2,1)} %convolution_convert_fusion.values, f32[16,8,128]{2,1,0:T(8,128)} %pad.4.stats), custom_call_target="tpu_custom_call" | custom-call | tf_op jit(solution)/shard_map/swap_partials/pallas_call | solution.py:117
  59.5 0.8 slice_bitcast_fusion.1
  60.4 0.2 copy.72
  60.6 1.2 mul.152
  61.9 1.9 mul.153
  63.8 2.2 %multiply_reduce_fusion = f32[64,512]{1,0:T(8,128)S(1)} fusion(f32[16,64,512]{2,1,0:T(8,128)} %mul.153, bf16[16,64,512]{2,1,0:T(8,128)(2,1)} %get-tuple-element.9), kind=kLoop, calls=%fused_computation.5 | loop fusion | flops 1540096 | bytes 3276800 | tf_op jit(solution)/shard_map/reduce_sum | solution.py:641
  66.1 0.2 fusion.41
  66.5 0.1 broadcast_multiply_fusion
  67.0 0.1 div.51
  67.2 0.2 fusion.66
  67.4 0.3 fusion.14
  67.8 3.9 %fusion.6.parts = bf16[8,128,512]{2,1,0:T(8,128)(2,1)} fusion(bf16[64,8,8,512]{3,2,1,0:T(8,128)(2,1)} %bitcast.147, bf16[64,512]{1,0:T(8,128)(2,1)S(1)} %bitcast.143, bf16[64,512]{1,0:T(8,128)(2,1)S(1)} %fusion.25), kind=kOutput, calls=%fused_computation.10 | convolution fusion | flops 537657344 | bytes 5373952 | tf_op jit(solution)/shard_map/th,hpc->ptc/dot_general | solution.py:680
  71.7 1.3 dynamic_slice.3
  73.1 26.0 %hidden_and_norm.1 = (f32[128,512]{1,0:T(8,128)}, bf16[128,512]{1,0:T(8,128)(2,1)}) custom-call(bf16[8,128,512]{2,1,0:T(8,128)(2,1)} %fusion.6.parts, bf16[128,512]{1,0:T(8,128)(2,1)} %residual.1, f32[1,512]{1,0:T(1,128)} %bitcast.144), custom_call_target="tpu_custom_call" | custom-call | tf_op jit(solution)/shard_map/hidden_and_norm/pallas_call | solution.py:162
  99.2 0.1 eq.133
  99.4 0.6 reduce-window.19
  100.0 0.2 slice_reduce_fusion.1
  100.2 0.1 eq.129
  100.5 0.1 reduce_sum.113
  100.8 1.2 convolution_convert_fusion.1
  102.1 1.0 broadcast_in_dim.149
  103.0 77.2 %experts.1 = bf16[3,16,16,512]{3,2,1,0:T(8,128)(2,1)} custom-call(bf16[3,16,16,512]{3,2,1,0:T(8,128)(2,1)} %bitcast.134, bf16[4096,768]{1,0:T(8,128)(2,1)} %wg.1, bf16[4096,768]{1,0:T(8,128)(2,1)} %wu.1, bf16[768,4096]{1,0:T(8,128)(2,1)} %wd.1), custom_call_target="tpu_custom_call" | custom-call | tf_op jit(solution)/shard_map/experts/pallas_call | solution.py:457
  180.2 1.4 convert_reduce_fusion
  181.6 0.1 select_reduce_fusion.4
  181.8 1.3 convolution_add_fusion.mixed
  183.1 14.6 %closing_norm.1 = bf16[128,512]{1,0:T(8,128)(2,1)} custom-call(f32[128,512]{1,0:T(8,128)} %convolution_add_fusion.mixed, f32[1,512]{1,0:T(1,128)} %bitcast.145), custom_call_target="tpu_custom_call" | custom-call | tf_op jit(solution)/shard_map/closing_norm/pallas_call | solution.py:524
  197.7 1.6 copy.121
  (57 shorter events, 1.9 us)
Async XLA Ops:
  0.0 34.3 %copy-start = (bf16[128,16,128]{2,1,0:T(8,128)(2,1)S(1)}, bf16[128,16,128]{2,1,0:T(8,128)(2,1)}, u32[]{:S(2)}) copy-start(bf16[128,16,128]{2,1,0:T(8,128)(2,1)} %param.21) | copy-start | bytes 1572868
  0.0 30.4 %copy-start.2 = (bf16[128,16,128]{2,1,0:T(8,128)(2,1)S(1)}, bf16[128,16,128]{2,1,0:T(8,128)(2,1)}, u32[]{:S(2)}) copy-start(bf16[128,16,128]{2,1,0:T(8,128)(2,1)} %param.20) | copy-start | bytes 1572868
  63.8 2.2 %copy-start.1 = (bf16[64,512]{1,0:T(8,128)(2,1)S(1)}, bf16[64,512]{1,0:T(8,128)(2,1)}, u32[]{:S(2)}) copy-start(bf16[64,512]{1,0:T(8,128)(2,1)} %get-tuple-element.22.src) | copy-start | bytes 196612
  63.8 2.3 %copy-start.4 = (bf16[128,128]{1,0:T(8,128)(2,1)S(1)}, bf16[128,128]{1,0:T(8,128)(2,1)}, u32[]{:S(2)}) copy-start(bf16[128,128]{1,0:T(8,128)(2,1)} %param.18) | copy-start | bytes 98308
  63.8 2.7 %copy-start.5 = (bf16[128,128]{1,0:T(8,128)(2,1)S(1)}, bf16[128,128]{1,0:T(8,128)(2,1)}, u32[]{:S(2)}) copy-start(bf16[128,128]{1,0:T(8,128)(2,1)} %param.19) | copy-start | bytes 98308
  67.8 31.3 %copy-start.6 = (s32[128,2]{0,1:T(2,128)S(1)}, s32[128,2]{0,1:T(2,128)}, u32[]{:S(2)}) copy-start(s32[128,2]{0,1:T(2,128)} %param.26) | copy-start | bytes 3076
  103.0 78.6 %copy-start.7 = (f32[128,2]{0,1:T(2,128)S(1)}, f32[128,2]{0,1:T(2,128)}, u32[]{:S(2)}) copy-start(f32[128,2]{0,1:T(2,128)} %param.27) | copy-start | bytes 3076
  103.0 78.7 %copy-start.3 = (f32[128,512]{1,0:T(8,128)S(1)}, f32[128,512]{1,0:T(8,128)}, u32[]{:S(2)}) copy-start(f32[128,512]{1,0:T(8,128)} %get-tuple-element.11) | copy-start | bytes 786436

commit v2 on v1

v2 whole, which is shorter than its diff:
```python
import functools

import jax
import jax.numpy as jnp
from jax import lax
from jax.experimental import pallas as pl
from jax.experimental.pallas import tpu as pltpu
from jax.sharding import PartitionSpec as P

D = 4096
HQ = 32
KVH = 8
HD = 128
E = 8
PAGE = 16
DEC = 64
PRE = 64
C = 48
NDP = 16
NCH = 3
SL = C // NCH
RC = NDP * SL
FW = 512
HID = 768

MESH = pl.DeviceIdType.MESH
DMA = pltpu.SemaphoreType.DMA
BF = jnp.bfloat16
F32 = jnp.float32

neg_big = -1e30
eps_norm = 1e-05


def remote(src, dst, send_sem, recv_sem, device):
    return pltpu.make_async_remote_copy(
        src_ref=src,
        dst_ref=dst,
        send_sem=send_sem,
        recv_sem=recv_sem,
        device_id=device,
        device_id_type=MESH,
    )


def greet(devices):
    barrier = pltpu.get_barrier_semaphore()
    for device in devices:
        pl.semaphore_signal(barrier, inc=1, device_id=device, device_id_type=MESH)
    pl.semaphore_wait(barrier, len(devices))


def comm_params(collective_id):
    return pltpu.CompilerParams(
        collective_id=collective_id, has_side_effects=True, vmem_limit_bytes=60 << 20
    )


def vmem(count):
    return [pl.BlockSpec(memory_space=pltpu.VMEM)] * count


def iota(shape, axis):
    return lax.broadcasted_iota(jnp.int32, shape, axis)


def square_sums(rows):
    ones = jnp.ones((8, FW), F32)
    return lax.dot_general(
        ones,
        rows * rows,
        (((1,), (1,)), ((), ())),
        precision=lax.Precision.HIGHEST,
        preferred_element_type=F32,
    )


def as_columns(row):
    wide = jnp.broadcast_to(row[0:1, :], (128, 128)).T
    return jnp.concatenate([wide] * (FW // 128), axis=1)


def to_columns(stack):
    return stack.T


def attend_kernel(
    queries,
    new_keys,
    new_values,
    keys,
    values,
    lengths,
    order,
    out_proj,
    residual,
    gain,
    routes,
    send,
    hidden,
    picks,
    q_all,
    keys_v,
    values_v,
    proj_v,
    owners,
    scores,
    weights,
    page_q,
    page_w,
    val_out,
    val_in,
    stat_out,
    stat_in,
    attn,
    part,
    got,
    squares,
    l_sems,
    s1,
    r1,
    s2,
    r2,
    vs,
    vr,
    ts,
    tr,
    ps,
    pr,
    qs,
    qr,
):
    dp = lax.axis_index("dp")
    mp = lax.axis_index("mp")
    z, y = dp // 4, lax.rem(dp, 4)
    scale = HD ** (-0.5)
    dp_peers = [lax.rem(dp + k, NDP) for k in range(1, NDP)]
    mp_peers = [lax.rem(mp + k, 8) for k in range(1, 8)]
    loads = [
        pltpu.make_async_copy(keys, keys_v, l_sems.at[0]),
        pltpu.make_async_copy(values, values_v, l_sems.at[1]),
        pltpu.make_async_copy(out_proj, proj_v, l_sems.at[2]),
    ]
    q_rows = DEC // 2

    def q_half(owner, h):
        return q_all.at[pl.ds(pl.multiple_of(owner * DEC + h * q_rows, q_rows), q_rows), :]

    own_q = pltpu.make_async_copy(
        queries.at[pl.ds(0, DEC), :],
        q_all.at[pl.ds(pl.multiple_of(dp * DEC, DEC), DEC), :],
        l_sems.at[3],
    )
    own_q.start()
    loads[2].start()
    loads[0].start()
    loads[1].start()
    own_q.wait()
    greet([{"dp": p} for p in dp_peers] + [{"mp": p} for p in mp_peers])
    sent = []

    def go(copy):
        copy.start()
        sent.append(copy)

    def group(along, step, across):
        zz = lax.rem(z + (step if along == 0 else across) + 8, 4)
        yy = lax.rem(y + (across if along == 0 else step) + 8, 4)
        return zz * 4 + yy

    def first(h, k):
        return remote(q_half(dp, h), q_half(dp, h), s1.at[h, k - 1], r1.at[h, k - 1], {"dp": group(h, k, 0)})

    def second(h, j, k):
        owner = group(h, -j, 0)
        return remote(
            q_half(owner, h), q_half(owner, h), s2.at[h, j, k - 1], r2.at[h, j, k - 1], {"dp": group(h, 0, k)}
        )

    for k in (1, 3, 2):
        for h in range(2):
            go(first(h, k))
    for h in range(2):
        for k in range(1, 4):
            go(second(h, 0, k))

    lane = iota((128, 128), 1)
    row = iota((128, 128), 0)
    counts = lax.shift_right_logical(lengths[...] + (PAGE - 1), 4)
    upto = (row <= lane).astype(BF)
    within = jnp.dot(counts.astype(F32).astype(BF), upto, preferred_element_type=F32)
    place = jnp.zeros((128, 128), F32)
    ids = dp * 128 + row
    for q in range(16):
        place = place + jnp.where(order[q : q + 1, :] == ids, (lane + q * 128).astype(F32), 0.0)
    place = jnp.sum(place, axis=1, keepdims=True)
    before = jnp.zeros((1, 1), F32)
    passed = jnp.zeros((128, 128), F32)
    ends = []
    for i in range(8):
        ends.append(within[i : i + 1, :] + before)
        before = before + within[i : i + 1, 127:128]
        passed = passed + jnp.where(ends[i] <= place, 1.0, 0.0)
    owner = jnp.sum(passed, axis=1, keepdims=True)

    for k in range(1, 4):
        for h in range(2):
            remote(q_half(dp, h), q_half(group(h, -k, 0), h), s1.at[h, k - 1], r1.at[h, k - 1], {"dp": dp_peers[0]}).wait_recv()
            for kk in range(1, 4):
                go(second(h, k, kk))

    begin = jnp.zeros((128, 128), F32)
    length = jnp.zeros((128, 128), F32)
    for i in range(8):
        mine = (lane + i * 128).astype(F32) == owner
        cnt = counts[i : i + 1, :].astype(F32)
        begin = begin + jnp.where(mine, ends[i] - cnt, 0.0)
        length = length + jnp.where(mine, lengths[i : i + 1, :].astype(F32), 0.0)
        owners[:, i * 128 : (i + 1) * 128] = jnp.where(mine, 1.0, 0.0).astype(BF)
    begin = jnp.sum(begin, axis=1, keepdims=True)
    length = jnp.sum(length, axis=1, keepdims=True)
    valid = length - (place - begin) * PAGE
    key_ok = (lax.shift_right_logical(lane, 4) == (row & 7)) & ((lane & 15).astype(F32) < valid)
    owner_row = jnp.broadcast_to(owner, (128, 128)).T
    same = owner_row == owner
    leader = jnp.sum(jnp.where(same & (lane < row), 1.0, 0.0), axis=1, keepdims=True) == 0.0

    below = (lane < row).astype(BF)
    route = [routes[:, 0:1], routes[:, 1:2]]
    named = [(lane == r).astype(F32) for r in route]
    ahead = [jnp.dot(below, n.astype(BF), preferred_element_type=F32) for n in named]
    ahead[1] = ahead[1] + jnp.sum(named[0], axis=0, keepdims=True)
    cells = iota((128, E * C), 1)
    for k in range(2):
        slot = jnp.sum(named[k] * ahead[k], axis=1, keepdims=True).astype(jnp.int32)
        target = lax.shift_right_logical(slot, 4) * (E * SL) + route[k] * SL + (slot & (SL - 1))
        picks[k] = jnp.where(cells == target, 1.0, 0.0).astype(BF)

    causal = iota((PRE, PRE), 0) >= iota((PRE, PRE), 1)
    for g in range(4):
        cols = slice(g * HD, (g + 1) * HD)
        s = lax.dot_general(
            queries[DEC:, cols], new_keys[DEC:, :], (((1,), (1,)), ((), ())), preferred_element_type=F32
        )
        s = jnp.where(causal, s * scale, neg_big)
        w = jnp.where(causal, jnp.exp(s - jnp.max(s, axis=1, keepdims=True)), 0.0)
        den = jnp.sum(w, axis=1, keepdims=True)
        num = jnp.dot(w.astype(BF), new_values[DEC:, :], preferred_element_type=F32)
        attn[DEC:, cols] = (num / den).astype(BF)
    loads[2].wait()

    def project(t):
        rows = slice(t * 64, (t + 1) * 64)
        a = attn[rows, :]
        for k, p in enumerate(mp_peers):
            cols = pl.ds(pl.multiple_of(p * FW, FW), FW)
            part[t, k] = jnp.dot(a, proj_v[:, cols], preferred_element_type=F32).astype(BF)
            go(remote(part.at[t, k], got.at[t, k], ps.at[t, k], pr.at[t, k], {"mp": p}))
        cols = pl.ds(pl.multiple_of(mp * FW, FW), FW)
        own = jnp.dot(a, proj_v[:, cols], preferred_element_type=F32)
        hidden[rows, :] = own + residual[rows, :].astype(F32)

    def collect(t):
        rows = slice(t * 64, (t + 1) * 64)
        total = hidden[rows, :]
        for k in range(7):
            remote(part.at[t, k], got.at[t, k], ps.at[t, k], pr.at[t, k], {"mp": mp_peers[k]}).wait_recv()
            total = total + got[t, k].astype(F32)
        hidden[rows, :] = total

    project(1)

    own_cols = jnp.zeros((64, 128), F32)
    lane64 = iota((64, 128), 1)
    for g in range(4):
        prod = queries[:DEC, g * HD : (g + 1) * HD].astype(F32) * new_keys[:DEC, :].astype(F32)
        own_cols = jnp.where(lane64 == g, jnp.sum(prod, axis=1, keepdims=True) * scale, own_cols)
    own_score = to_columns(jnp.concatenate([own_cols, jnp.zeros((64, 128), F32)], axis=0))[0:8, :]

    for j in range(4):
        for k in range(1, 4):
            for h in range(2):
                remote(
                    q_half(dp, h), q_half(group(h, -j, -k), h), s2.at[h, j, k - 1], r2.at[h, j, k - 1], {"dp": dp_peers[0]}
                ).wait_recv()

    page_q[...] = jnp.dot(owners[...], q_all[...], preferred_element_type=F32)
    loads[0].wait()
    loads[1].wait()
    for k in range(16):
        qk = jnp.concatenate([page_q[8 * k : 8 * k + 8, g * HD : (g + 1) * HD] for g in range(4)], axis=0)
        s = lax.dot_general(
            qk.astype(BF), keys_v[128 * k : 128 * (k + 1), :], (((1,), (1,)), ((), ())), preferred_element_type=F32
        )
        for g in range(4):
            scores[g, 8 * k : 8 * k + 8, :] = s[8 * g : 8 * g + 8, :]
    tops = jnp.zeros((128, 128), F32)
    sums = []
    for g in range(4):
        s = jnp.where(key_ok, scores[g] * scale, neg_big)
        m = jnp.max(s, axis=1, keepdims=True)
        w = jnp.where(key_ok, jnp.exp(s - m), 0.0)
        weights[g] = w
        sums.append(jnp.sum(w, axis=1, keepdims=True))
        tops = jnp.where(lane == g, m, tops)
    for k in range(16):
        wk = jnp.concatenate([weights[g, 8 * k : 8 * k + 8, :] for g in range(4)], axis=0)
        v = jnp.dot(wk.astype(BF), values_v[128 * k : 128 * (k + 1), :], preferred_element_type=F32)
        for g in range(4):
            scores[g, 8 * k : 8 * k + 8, :] = v[8 * g : 8 * g + 8, :]
    top_rows = tops.T
    stat = jnp.zeros((128, 128), F32)
    for g in range(4):
        top = jnp.max(jnp.where(same, top_rows[g : g + 1, :], neg_big), axis=1, keepdims=True)
        factor = jnp.exp(tops[:, g : g + 1] - top)
        page_w[:, g * HD : (g + 1) * HD] = (scores[g] * factor).astype(BF)
        stat = jnp.where(lane == g, jnp.where(leader, top, 0.0), stat)
        stat = jnp.where(lane == 4 + g, sums[g] * factor, stat)
    stat8 = stat.T[0:8, :]
    for i in range(8):
        stat_out[i] = jnp.dot(
            stat8,
            owners[:, i * 128 : (i + 1) * 128].astype(F32),
            precision=lax.Precision.HIGHEST,
            preferred_element_type=F32,
        )
    for i in range(4):
        val_out[i * 256 : (i + 1) * 256, :] = lax.dot_general(
            owners[:, i * 256 : (i + 1) * 256], page_w[...], (((0,), (0,)), ((), ())), preferred_element_type=F32
        ).astype(BF)

    def val_rows(p):
        return val_out.at[pl.ds(pl.multiple_of(p * DEC, DEC), DEC), :]

    def swap_stat(k):
        p = dp_peers[k]
        return remote(stat_out.at[p // 2], stat_in.at[k], ts.at[k], tr.at[k], {"dp": p})

    def swap_val(k):
        p = dp_peers[k]
        return remote(val_rows(p), val_in.at[k], vs.at[k], vr.at[k], {"dp": p})

    for k in range(NDP - 1):
        go(swap_stat(k))
        go(swap_val(k))

    collect(1)
    for k in range(NDP - 1):
        swap_stat(k).wait_recv()
    stat_in[NDP - 1] = stat_out[dp // 2]
    odd = lax.rem(dp, 2) == 1
    got_stats = stat_in[...].reshape(128, 128)
    got_stats = jnp.where(odd, pltpu.roll(got_stats, 64, 1), got_stats).reshape(NDP, 8, 128)
    l_in = pltpu.roll(got_stats, 4, 1)
    m_in = jnp.where(l_in > 0.0, got_stats, neg_big)
    top = jnp.maximum(jnp.max(m_in, axis=0), own_score)
    f_in = jnp.where(l_in > 0.0, jnp.exp(jnp.minimum(m_in - top[None], 0.0)), 0.0)
    f_own = jnp.exp(own_score - top)
    inv = 1.0 / (jnp.sum(l_in * f_in, axis=0) + f_own)
    f_cols = to_columns((f_in * inv[None]).reshape(128, 128))
    own_f = to_columns(jnp.concatenate([f_own * inv, jnp.zeros((120, 128), F32)], axis=0))
    nums = [own_f[:DEC, g : g + 1] * new_values[:DEC, :].astype(F32) for g in range(4)]
    mine = val_out[pl.ds(pl.multiple_of(dp * DEC, DEC), DEC), :]
    for k in range(NDP):
        if k < NDP - 1:
            swap_val(k).wait_recv()
        v = (val_in[k] if k < NDP - 1 else mine).astype(F32)
        for g in range(4):
            nums[g] = nums[g] + v[:, g * HD : (g + 1) * HD] * f_cols[:DEC, 8 * k + g : 8 * k + g + 1]
    for g in range(4):
        attn[:DEC, g * HD : (g + 1) * HD] = nums[g].astype(BF)
    project(0)
    collect(0)

    squares[7] = square_sums(hidden[...])
    for k, p in enumerate(mp_peers):
        go(remote(squares.at[7], squares.at[k], qs.at[k], qr.at[k], {"mp": p}))
    summed = squares[7]
    for k, p in enumerate(mp_peers):
        remote(squares.at[7], squares.at[k], qs.at[k], qr.at[k], {"mp": p}).wait_recv()
        summed = summed + squares[k]
    normed = (hidden[...] * as_columns(lax.rsqrt(summed / D + eps_norm)) * gain[...]).astype(BF)
    dispatch = picks[0] + picks[1]
    for ch in range(NCH):
        rows = lax.dot_general(
            dispatch[:, ch * 128 : (ch + 1) * 128], normed, (((0,), (0,)), ((), ())), preferred_element_type=F32
        ).astype(BF)
        send[ch] = rows.reshape(E, SL, FW)
    for copy in sent:
        copy.wait_send()


def attend(queries, new_keys, new_values, keys, values, lengths, order, out_proj, residual, gain, routes, collective_id):
    anyspace = pl.BlockSpec(memory_space=pl.ANY)
    return pl.pallas_call(
        attend_kernel,
        out_shape=(
            jax.ShapeDtypeStruct((NCH, E, SL, FW), BF),
            jax.ShapeDtypeStruct((128, FW), F32),
            jax.ShapeDtypeStruct((2, 128, E * C), BF),
        ),
        in_specs=vmem(3) + [anyspace] * 2 + vmem(2) + [anyspace] + vmem(3),
        out_specs=tuple(vmem(3)),
        scratch_shapes=[
            pltpu.VMEM((NDP * DEC, FW), BF),
            pltpu.VMEM((2048, HD), BF),
            pltpu.VMEM((2048, HD), BF),
            pltpu.VMEM((FW, D), BF),
            pltpu.VMEM((128, NDP * DEC), BF),
            pltpu.VMEM((4, 128, 128), F32),
            pltpu.VMEM((4, 128, 128), F32),
            pltpu.VMEM((128, FW), F32),
            pltpu.VMEM((128, FW), BF),
            pltpu.VMEM((NDP * DEC, FW), BF),
            pltpu.VMEM((NDP - 1, DEC, FW), BF),
            pltpu.VMEM((8, 8, 128), F32),
            pltpu.VMEM((NDP, 8, 128), F32),
            pltpu.VMEM((128, FW), BF),
            pltpu.VMEM((2, 7, 64, FW), BF),
            pltpu.VMEM((2, 7, 64, FW), BF),
            pltpu.VMEM((8, 8, 128), F32),
            DMA((4,)),
            DMA((2, 3)),
            DMA((2, 3)),
            DMA((2, 4, 3)),
            DMA((2, 4, 3)),
            DMA((NDP - 1,)),
            DMA((NDP - 1,)),
            DMA((NDP - 1,)),
            DMA((NDP - 1,)),
            DMA((2, 7)),
            DMA((2, 7)),
            DMA((7,)),
            DMA((7,)),
        ],
        compiler_params=comm_params(collective_id),
        name="attend",
    )(queries, new_keys, new_values, keys, values, lengths, order, out_proj, residual, gain, routes)


def experts_kernel(
    send,
    wg,
    wu,
    wd,
    ret,
    x_all,
    wg_v,
    wu_v,
    wd_v,
    hid,
    part,
    own_part,
    hop_in,
    hop_out,
    fin,
    out,
    w_sems,
    wp_send,
    wp_recv,
    a_send,
    a_recv,
    a_own,
    g_send,
    g_recv,
    f_send,
    f_recv,
    p_send,
    p_recv,
    h_send,
    h_recv,
    t_send,
    t_recv,
    n_send,
    n_recv,
    r_send,
    r_recv,
    r_own,
):
    dp = lax.axis_index("dp")
    mp = lax.axis_index("mp")
    x, c = mp // 2, lax.rem(mp, 2)
    xr, xo, xl = lax.rem(x + 1, 4), lax.rem(x + 2, 4), lax.rem(x + 3, 4)
    mr, mo, ml = xr * 2 + c, xo * 2 + c, xl * 2 + c
    right, left, mate = {"mp": mr}, {"mp": ml}, {"mp": x * 2 + 1 - c}
    sides = (right, left)
    peers = [lax.rem(dp + k, NDP) for k in range(1, NDP)]
    half = RC // 2

    w_copies = [
        pltpu.make_async_copy(wg, wg_v, w_sems.at[0]),
        pltpu.make_async_copy(wu, wu_v, w_sems.at[1]),
    ]
    for j in range(4):
        w_copies.append(
            pltpu.make_async_copy(
                wd.at[:, pl.ds(pl.multiple_of(j * 1024 + c * FW, FW), FW)],
                wd_v.at[0, :, pl.ds(j * FW, FW)],
                w_sems.at[2 + j],
            )
        )
    greet([{"dp": p} for p in peers] + [right, left, mate])

    def columns(owner):
        return pl.ds(pl.multiple_of(owner * FW, FW), FW)

    sent = []

    def go(copy):
        copy.start()
        sent.append(copy)

    out_copies, own_copies = [], []
    for ch in range(NCH):
        rows = pl.ds(pl.multiple_of(dp * SL, SL), SL)
        own = pltpu.make_async_copy(send.at[ch, dp // 2], x_all.at[ch, rows, columns(mp)], a_own.at[ch])
        own.start()
        own_copies.append(own)
        cs = []
        for k, p in enumerate(peers):
            copy = remote(
                send.at[ch, p // 2],
                x_all.at[ch, rows, columns(mp)],
                a_send.at[ch, k],
                a_recv.at[ch, k],
                {"dp": p},
            )
            go(copy)
            cs.append(copy)
        out_copies.append(cs)
    for copy in w_copies:
        copy.start()
    mate_w = []
    for j in range(4):
        mate_w.append(
            remote(
                wd.at[:, pl.ds(pl.multiple_of(j * 1024 + (1 - c) * FW, FW), FW)],
                wd_v.at[1, :, pl.ds(j * FW, FW)],
                wp_send.at[j],
                wp_recv.at[j],
                mate,
            )
        )
        go(mate_w[j])

    def block(ch, h, owner):
        return x_all.at[ch, pl.ds(h * half, half), columns(owner)]

    def whole(ch, owner):
        return x_all.at[ch, :, columns(owner)]

    def neighbour(ch, side, h):
        return remote(block(ch, h, mp), block(ch, h, mp), g_send.at[ch, side, h], g_recv.at[ch, side, h], sides[side])

    def onward(ch, side):
        owner = (ml, mr)[side]
        return remote(
            block(ch, side, owner), block(ch, side, owner), f_send.at[ch, side], f_recv.at[ch, side], sides[side]
        )

    def to_mate(ch, which):
        owner = (mp, ml, mr, mo)[which]
        return remote(whole(ch, owner), whole(ch, owner), p_send.at[ch, which], p_recv.at[ch, which], mate)

    def spread_own(ch):
        for copy in out_copies[ch]:
            copy.wait_recv()
        own_copies[ch].wait()
        for h in range(2):
            go(neighbour(ch, 0, h))
            go(neighbour(ch, 1, 1 - h))
        go(to_mate(ch, 0))

    def spread_on(ch):
        for side in range(2):
            neighbour(ch, side, side).wait_recv()
            go(onward(ch, side))

    def spread_rest(ch):
        for side in range(2):
            neighbour(ch, side, 1 - side).wait_recv()
            go(to_mate(ch, 1 + side))

    def spread_far(ch):
        for side in range(2):
            onward(ch, side).wait_recv()
        go(to_mate(ch, 3))

    def spread_end(ch):
        for which in range(4):
            to_mate(ch, which).wait_recv()

    def hidden_send(ch):
        return remote(hid.at[ch, 0], hid.at[ch, 1], h_send.at[ch], h_recv.at[ch], mate)

    def gate_up(ch, n):
        cols = pl.ds(n * 256, 256)
        rows = x_all[ch]
        g = jnp.dot(rows, wg_v[:, cols], preferred_element_type=F32)
        u = jnp.dot(rows, wu_v[:, cols], preferred_element_type=F32)
        hid[ch, 0, :, cols] = (g / (1.0 + jnp.exp(-g)) * u).astype(BF)

    def down(ch, owner):
        cols = columns(owner)
        return jnp.dot(hid[ch, 0], wd_v[0, :, cols], preferred_element_type=F32) + jnp.dot(
            hid[ch, 1], wd_v[1, :, cols], preferred_element_type=F32
        )

    def rows_of(h):
        return pl.ds(h * half, half)

    def hop(ch, side):
        return remote(
            part.at[ch, 0, rows_of(side)], hop_in.at[ch, side], t_send.at[ch, side], t_recv.at[ch, side], sides[side]
        )

    def near(ch, side, h, src):
        return remote(src, fin.at[ch, side, rows_of(h)], n_send.at[ch, side, h], n_recv.at[ch, side, h], sides[side])

    def reduce_start(ch):
        part[ch, 0] = down(ch, xo).astype(BF)
        for side in range(2):
            go(hop(ch, side))
        for side in range(2):
            part[ch, 1 + side] = down(ch, (xr, xl)[side]).astype(BF)
            go(near(ch, side, 1 - side, part.at[ch, 1 + side, rows_of(1 - side)]))

    def reduce_own(ch):
        own_part[ch] = down(ch, x)

    def reduce_hop(ch):
        for side in range(2):
            hop(ch, side).wait_recv()
            hop_out[ch, side] = (
                part[ch, 1 + side, rows_of(side), :].astype(F32) + hop_in[ch, side].astype(F32)
            ).astype(BF)
            go(near(ch, side, side, hop_out.at[ch, side]))

    ret_copies = []

    def reduce_end(ch):
        for side in range(2):
            for h in range(2):
                near(ch, side, h, hop_out.at[ch, side]).wait_recv()
        total = own_part[ch] + fin[ch, 0].astype(F32) + fin[ch, 1].astype(F32)
        out[ch] = total.astype(BF)
        own = pltpu.make_async_copy(
            out.at[ch, pl.ds(pl.multiple_of(dp * SL, SL), SL)], ret.at[ch, dp], r_own.at[ch]
        )
        own.start()
        cs = [own]
        for k, p in enumerate(peers):
            copy = remote(
                out.at[ch, pl.ds(pl.multiple_of(p * SL, SL), SL)],
                ret.at[ch, dp],
                r_send.at[ch, k],
                r_recv.at[ch, k],
                {"dp": p},
            )
            copy.start()
            cs.append(copy)
        ret_copies.extend(cs)

    spread_own(0)
    spread_on(0)
    spread_own(1)
    spread_rest(0)
    spread_far(0)
    for copy in w_copies[:2]:
        copy.wait()
    spread_on(1)
    spread_own(2)
    spread_end(0)
    for ch in range(NCH):
        gate_up(ch, 0)
        if ch == 0:
            spread_rest(1)
        if ch == 1:
            reduce_hop(0)
        if ch == 2:
            reduce_hop(1)
        gate_up(ch, 1)
        if ch == 0:
            spread_far(1)
        if ch == 1:
            spread_rest(2)
        gate_up(ch, 2)
        go(hidden_send(ch))
        if ch == 0:
            spread_on(2)
            for copy in w_copies[2:]:
                copy.wait()
            for copy in mate_w:
                copy.wait_recv()
        if ch == 1:
            spread_far(2)
            reduce_end(0)
        if ch == 2:
            reduce_end(1)
        hidden_send(ch).wait_recv()
        reduce_start(ch)
        reduce_own(ch)
        if ch < 2:
            spread_end(ch + 1)
    reduce_hop(2)
    reduce_end(2)
    for copy in ret_copies:
        copy.wait()
    for copy in sent:
        copy.wait_send()


def experts(send, wg, wu, wd, collective_id):
    anyspace = pl.BlockSpec(memory_space=pl.ANY)
    return pl.pallas_call(
        experts_kernel,
        out_shape=jax.ShapeDtypeStruct((NCH, NDP, SL, FW), BF),
        in_specs=vmem(1) + [anyspace] * 3,
        out_specs=vmem(1)[0],
        scratch_shapes=[
            pltpu.VMEM((NCH, RC, D), BF),
            pltpu.VMEM((D, HID), BF),
            pltpu.VMEM((D, HID), BF),
            pltpu.VMEM((2, HID, D // 2), BF),
            pltpu.VMEM((NCH, 2, RC, HID), BF),
            pltpu.VMEM((NCH, 3, RC, FW), BF),
            pltpu.VMEM((NCH, RC, FW), F32),
            pltpu.VMEM((NCH, 2, RC // 2, FW), BF),
            pltpu.VMEM((NCH, 2, RC // 2, FW), BF),
            pltpu.VMEM((NCH, 2, RC, FW), BF),
            pltpu.VMEM((NCH, RC, FW), BF),
            DMA((6,)),
            DMA((4,)),
            DMA((4,)),
            DMA((NCH, NDP - 1)),
            DMA((NCH, NDP - 1)),
            DMA((NCH,)),
            DMA((NCH, 2, 2)),
            DMA((NCH, 2, 2)),
            DMA((NCH, 2)),
            DMA((NCH, 2)),
            DMA((NCH, 4)),
            DMA((NCH, 4)),
            DMA((NCH,)),
            DMA((NCH,)),
            DMA((NCH, 2)),
            DMA((NCH, 2)),
            DMA((NCH, 2, 2)),
            DMA((NCH, 2, 2)),
            DMA((NCH, NDP - 1)),
            DMA((NCH, NDP - 1)),
            DMA((NCH,)),
        ],
        compiler_params=comm_params(collective_id),
        name="experts",
    )(send, wg, wu, wd)


def closing_kernel(ret, picks, weight, hidden, gain, out, squares, send, recv):
    me = lax.axis_index("mp")
    peers = [lax.rem(me + k, 8) for k in range(1, 8)]
    greet([{"mp": p} for p in peers])
    mixed = hidden[...]
    for k in range(2):
        rows = jnp.zeros((128, FW), F32)
        for j in range(2):
            back = ret[:, j].reshape(E * C, FW)
            rows = rows + jnp.dot(picks[k], back, preferred_element_type=F32)
        mixed = mixed + weight[:, k : k + 1] * rows
    squares[7] = square_sums(mixed)
    copies = []
    for k, p in enumerate(peers):
        copies.append(remote(squares.at[7], squares.at[k], send.at[k], recv.at[k], {"mp": p}))
        copies[-1].start()
    summed = squares[7]
    for k, copy in enumerate(copies):
        copy.wait_recv()
        summed = summed + squares[k]
    out[...] = (mixed * as_columns(lax.rsqrt(summed / D + eps_norm)) * gain[...]).astype(BF)
    for copy in copies:
        copy.wait_send()


def closing_norm(ret, picks, weight, hidden, gain, collective_id):
    return pl.pallas_call(
        closing_kernel,
        out_shape=jax.ShapeDtypeStruct((128, FW), BF),
        in_specs=vmem(5),
        out_specs=vmem(1)[0],
        scratch_shapes=[pltpu.VMEM((8, 8, 128), F32), DMA((7,)), DMA((7,))],
        compiler_params=comm_params(collective_id),
        name="closing_norm",
    )(ret, picks, weight, hidden, gain)


def local(
    residual,
    queries,
    new_keys,
    new_values,
    cache_keys,
    cache_values,
    cache_len,
    page_order,
    out_proj,
    attn_gain,
    routes,
    route_weight,
    gate_proj,
    up_proj,
    down_proj,
    final_gain,
):
    column_start = lax.axis_index("mp") * FW
    gain_cols = lax.dynamic_slice_in_dim(attn_gain, column_start, FW, 0)
    send, hidden, picks = attend(
        queries,
        new_keys,
        new_values,
        cache_keys.reshape(-1, HD),
        cache_values.reshape(-1, HD),
        cache_len.reshape(8, 128),
        page_order.reshape(16, 128),
        out_proj,
        residual,
        gain_cols[None, :],
        routes,
        0,
    )
    returned = experts(send, gate_proj, up_proj, down_proj, 1)
    return closing_norm(
        returned.reshape(NCH * E, 2, SL, FW), picks, route_weight, hidden, final_gain[None, :], 2
    )


def solution(mesh):
    return jax.shard_map(
        local,
        mesh=mesh,
        in_specs=(
            P("dp", "mp"),
            P("dp", "mp"),
            P("dp", "mp"),
            P("dp", "mp"),
            P("dp", None, "mp"),
            P("dp", None, "mp"),
            P(),
            P(),
            P("mp", None),
            P(),
            P("dp", None),
            P("dp", None),
            P(None, ("dp", "mp")),
            P(None, ("dp", "mp")),
            P(("dp", "mp"), None),
            P("mp"),
        ),
        out_specs=P("dp", "mp"),
        check_vma=False,
    )
```

time: 200 us -> 143 us (0.71)
  Pallas kernels: 163 us -> 137 us
  matrix products: 11.1 us -> 0 us
  local copies, waits for them, and re-layouts: 15.4 us -> 5.05 us
  other arithmetic: 9.8 us -> 0 us
    pallas_call x4 -> x2, Pallas kernels: 85.4 us -> 62.7 us  [the longest x1 50.9 us: attend(): pl.pallas_call(attend_kernel, out_shape=(jax.ShapeDtypeStruct((NCH, E, SL...]
    dot_general x10 -> x0, matrix products: 11.1 us -> none  [the longest x1 3.9 us: local(): jnp.einsum('th,hpc->ptc', attn, out_proj.reshape(FW, 8, FW), preferred_el...]
    reduce_sum x10 -> x0, other arithmetic: 6.39 us -> none  [the longest x1 2.22 us: local(): jnp.sum(weighted * factors[..., None], axis=0)]
    mul x3 -> x0, local copies, waits for them, and re-layouts: 3.27 us -> none  [the longest x2 3.15 us: local(): weighted * factors[..., None]]
    pallas_call x1, Pallas kernels: 77.2 us -> 74.5 us  [experts(): pl.pallas_call(experts_kernel, out_shape=jax.ShapeDtypeStruct((NCH, NDP,...]
    unnamed x19 -> x5, local copies, waits for them, and re-layouts: 1.73 us -> 3.73 us
where the time goes in v2:
time: 143 us; the launch traced here: 142 us
  Pallas kernels  137 us (96%)
  local copies, waits for them, and re-layouts  5.05 us (4%)
    pallas_call x1, Pallas kernels, experts(): pl.pallas_call(experts_kernel, out_shape=jax.ShapeDtypeStruct((NCH, NDP,...  74.5 us
    pallas_call x1, Pallas kernels, attend(): pl.pallas_call(attend_kernel, out_shape=(jax.ShapeDtypeStruct((NCH, E, SL...  50.9 us
    pallas_call x1, Pallas kernels, closing_norm(): pl.pallas_call(closing_kernel, out_shape=jax.ShapeDtypeStruct((128, FW),...  11.7 us
    unnamed x5, local copies, waits for them, and re-layouts  3.73 us

profile of v2, /device:TPU:1, one launch (start us, length us, event | category | flops | bytes accessed | tf_op | source)
XLA Modules:
  0.0 142.3 jit_solution(9566835452257818808)
XLA Ops:
  0.0 1.3 dynamic_slice.3
  1.3 1.4 copy.17.routes
  2.7 50.9 %attend.1 = (bf16[3,8,16,512]{3,2,1,0:T(8,128)(2,1)}, f32[128,512]{1,0:T(8,128)}, bf16[2,128,384]{2,1,0:T(8,128)(2,1)}) custom-call(bf16[128,512]{1,0:T(8,128)(2,1)} %queries.1, bf16[128,128]{1,0:T(8,128)(2,1)} %new_keys.1, bf16[128,128]{1,0:T(8,128)(2,1)} %new_values.1, bf16[2048,128]{1,0:T(8,128)(2,1)} %bitcast.8, bf16[2048,128]{1,0:T(8,128)(2,1)} %bitcast.9, ...), custom_call_target="tpu_custom_call" | custom-call | tf_op jit(solution)/shard_map/attend/pallas_call | solution.py:395
  53.7 0.0 copy-start
  53.7 74.5 %experts.1 = bf16[3,16,16,512]{3,2,1,0:T(8,128)(2,1)} custom-call(bf16[3,8,16,512]{3,2,1,0:T(8,128)(2,1)} %get-tuple-element.8.send, bf16[4096,768]{1,0:T(8,128)(2,1)} %wg.1, bf16[4096,768]{1,0:T(8,128)(2,1)} %wu.1, bf16[768,4096]{1,0:T(8,128)(2,1)} %wd.1), custom_call_target="tpu_custom_call" | custom-call | tf_op jit(solution)/shard_map/experts/pallas_call | solution.py:715
  128.2 0.0 copy-done
  128.2 0.7 copy.18.weight
  129.0 11.7 %closing_norm.1 = bf16[128,512]{1,0:T(8,128)(2,1)} custom-call(bf16[24,2,16,512]{3,2,1,0:T(8,128)(2,1)} %bitcast.7, bf16[2,128,384]{2,1,0:T(8,128)(2,1)} %get-tuple-element.9.picks, f32[128,2]{1,0:T(8,128)} %copy.18.weight, f32[128,512]{1,0:T(8,128)} %get-tuple-element.10.hidden, f32[1,512]{1,0:T(1,128)} %bitcast.13), custom_call_target="tpu_custom_call" | custom-call | tf_op jit(solution)/shard_map/closing_norm/pallas_call | solution.py:785
  140.7 1.6 %copy.20 = bf16[128,512]{1,0:T(8,128)(2,1)} copy(bf16[128,512]{1,0:T(8,128)(2,1)} %closing_norm.1) | data formatting | bytes 262144
Async XLA Ops:
  53.7 74.6 %copy-start = (f32[128,2]{0,1:T(2,128)S(1)}, f32[128,2]{0,1:T(2,128)}, u32[]{:S(2)}) copy-start(f32[128,2]{0,1:T(2,128)} %param.27) | copy-start | bytes 3076

commit v3 on v2

--- a/solution.py
+++ b/solution.py
@@ -18,6 +18,8 @@
 C = 48
 NDP = 16
 NCH = 3
+NA = 2
+NB = 2
 SL = C // NCH
 RC = NDP * SL
 FW = 512
@@ -97,6 +99,7 @@
     gain,
     routes,
     send,
+    normed_out,
     hidden,
     picks,
     q_all,
@@ -226,7 +229,9 @@
     leader = jnp.sum(jnp.where(same & (lane < row), 1.0, 0.0), axis=1, keepdims=True) == 0.0
 
     below = (lane < row).astype(BF)
-    route = [routes[:, 0:1], routes[:, 1:2]]
+    route = [
+        jnp.broadcast_to(routes[k : k + 1, :].astype(F32), (128, 128)).T[:, 0:1].astype(jnp.int32) for k in range(2)
+    ]
     named = [(lane == r).astype(F32) for r in route]
     ahead = [jnp.dot(below, n.astype(BF), preferred_element_type=F32) for n in named]
     ahead[1] = ahead[1] + jnp.sum(named[0], axis=0, keepdims=True)
@@ -379,9 +384,12 @@
     for k, p in enumerate(mp_peers):
         remote(squares.at[7], squares.at[k], qs.at[k], qr.at[k], {"mp": p}).wait_recv()
         summed = summed + squares[k]
-    normed = (hidden[...] * as_columns(lax.rsqrt(summed / D + eps_norm)) * gain[...]).astype(BF)
+    gain_rows = gain[pl.ds(mp * 4, 4), :]
+    gain_cols = jnp.concatenate([gain_rows[i : i + 1, :] for i in range(4)], axis=1)
+    normed = (hidden[...] * as_columns(lax.rsqrt(summed / D + eps_norm)) * gain_cols).astype(BF)
+    normed_out[...] = normed
     dispatch = picks[0] + picks[1]
-    for ch in range(NCH):
+    for ch in range(NA):
         rows = lax.dot_general(
             dispatch[:, ch * 128 : (ch + 1) * 128], normed, (((0,), (0,)), ((), ())), preferred_element_type=F32
         ).astype(BF)
@@ -395,12 +403,13 @@
     return pl.pallas_call(
         attend_kernel,
         out_shape=(
-            jax.ShapeDtypeStruct((NCH, E, SL, FW), BF),
+            jax.ShapeDtypeStruct((NA, E, SL, FW), BF),
+            jax.ShapeDtypeStruct((128, FW), BF),
             jax.ShapeDtypeStruct((128, FW), F32),
             jax.ShapeDtypeStruct((2, 128, E * C), BF),
         ),
         in_specs=vmem(3) + [anyspace] * 2 + vmem(2) + [anyspace] + vmem(3),
-        out_specs=tuple(vmem(3)),
+        out_specs=tuple(vmem(4)),
         scratch_shapes=[
             pltpu.VMEM((NDP * DEC, FW), BF),
             pltpu.VMEM((2048, HD), BF),
@@ -440,10 +449,15 @@
 
 def experts_kernel(
     send,
+    normed,
+    picks,
+    weight,
+    hidden,
+    gain,
     wg,
     wu,
     wd,
-    ret,
+    result,
     x_all,
     wg_v,
     wu_v,
@@ -455,6 +469,15 @@
     hop_out,
     fin,
     out,
+    ret,
+    tokens,
+    send_b,
+    part_b,
+    ret_b,
+    moe_out,
+    moe_in,
+    moe_own,
+    squares,
     w_sems,
     wp_send,
     wp_recv,
@@ -476,6 +499,12 @@
     r_send,
     r_recv,
     r_own,
+    k_send,
+    k_recv,
+    m_send,
+    m_recv,
+    q_send,
+    q_recv,
 ):
     dp = lax.axis_index("dp")
     mp = lax.axis_index("mp")
@@ -485,24 +514,42 @@
     right, left, mate = {"mp": mr}, {"mp": ml}, {"mp": x * 2 + 1 - c}
     sides = (right, left)
     peers = [lax.rem(dp + k, NDP) for k in range(1, NDP)]
+    mp_peers = [lax.rem(mp + k, 8) for k in range(1, 8)]
+    x_peers = [{"mp": lax.rem(x + k, 4) * 2 + c} for k in range(1, 4)]
     half = RC // 2
 
-    w_copies = [
-        pltpu.make_async_copy(wg, wg_v, w_sems.at[0]),
-        pltpu.make_async_copy(wu, wu_v, w_sems.at[1]),
-    ]
+    def wide(owner):
+        return pl.ds(pl.multiple_of((lax.rem(owner, 2) * 4 + owner // 2) * FW, FW), FW)
+
+    def columns(owner):
+        return pl.ds(pl.multiple_of(owner * FW, FW), FW)
+
+    dp_rows = pl.ds(pl.multiple_of(dp * SL, SL), SL)
+    c_cols = pl.ds(pl.multiple_of(c * 4 * FW, 4 * FW), 4 * FW)
+    mate_cols = pl.ds(pl.multiple_of((1 - c) * 4 * FW, 4 * FW), 4 * FW)
+
+    w_copies = []
+    for w, (src, dst) in enumerate(((wg, wg_v), (wu, wu_v))):
+        for core in range(2):
+            for chip in range(4):
+                w_copies.append(
+                    pltpu.make_async_copy(
+                        src.at[pl.ds((chip * 2 + core) * FW, FW), :],
+                        dst.at[pl.ds((core * 4 + chip) * FW, FW), :],
+                        w_sems.at[w * 8 + core * 4 + chip],
+                    )
+                )
     for j in range(4):
         w_copies.append(
             pltpu.make_async_copy(
                 wd.at[:, pl.ds(pl.multiple_of(j * 1024 + c * FW, FW), FW)],
                 wd_v.at[0, :, pl.ds(j * FW, FW)],
-                w_sems.at[2 + j],
+                w_sems.at[16 + j],
             )
         )
-    greet([{"dp": p} for p in peers] + [right, left, mate])
-
-    def columns(owner):
-        return pl.ds(pl.multiple_of(owner * FW, FW), FW)
+    own_tokens = pltpu.make_async_copy(normed, tokens.at[x], a_own.at[3])
+    own_tokens.start()
+    greet([{"dp": p} for p in peers] + [{"mp": p} for p in mp_peers])
 
     sent = []
 
@@ -510,20 +557,21 @@
         copy.start()
         sent.append(copy)
 
+    def token_copy(k):
+        return remote(normed, tokens.at[x], k_send.at[k], k_recv.at[k], x_peers[k])
+
+    for k in (0, 2, 1):
+        go(token_copy(k))
+
     out_copies, own_copies = [], []
-    for ch in range(NCH):
-        rows = pl.ds(pl.multiple_of(dp * SL, SL), SL)
-        own = pltpu.make_async_copy(send.at[ch, dp // 2], x_all.at[ch, rows, columns(mp)], a_own.at[ch])
+    for ch in range(NA):
+        own = pltpu.make_async_copy(send.at[ch, dp // 2], x_all.at[ch, dp_rows, wide(mp)], a_own.at[ch])
         own.start()
         own_copies.append(own)
         cs = []
         for k, p in enumerate(peers):
             copy = remote(
-                send.at[ch, p // 2],
-                x_all.at[ch, rows, columns(mp)],
-                a_send.at[ch, k],
-                a_recv.at[ch, k],
-                {"dp": p},
+                send.at[ch, p // 2], x_all.at[ch, dp_rows, wide(mp)], a_send.at[ch, k], a_recv.at[ch, k], {"dp": p}
             )
             go(copy)
             cs.append(copy)
@@ -541,13 +589,12 @@
                 mate,
             )
         )
-        go(mate_w[j])
 
     def block(ch, h, owner):
-        return x_all.at[ch, pl.ds(h * half, half), columns(owner)]
+        return x_all.at[ch, pl.ds(h * half, half), wide(owner)]
 
     def whole(ch, owner):
-        return x_all.at[ch, :, columns(owner)]
+        return x_all.at[ch, :, wide(owner)]
 
     def neighbour(ch, side, h):
         return remote(block(ch, h, mp), block(ch, h, mp), g_send.at[ch, side, h], g_recv.at[ch, side, h], sides[side])
@@ -590,6 +637,36 @@
         for which in range(4):
             to_mate(ch, which).wait_recv()
 
+    def whole_copy(k):
+        p = peers[k]
+        return remote(send_b.at[p // 2], x_all.at[2, dp_rows, c_cols], a_send.at[2, k], a_recv.at[2, k], {"dp": p})
+
+    def whole_own():
+        return pltpu.make_async_copy(send_b.at[dp // 2], x_all.at[2, dp_rows, c_cols], a_own.at[2])
+
+    def whole_mate():
+        return remote(x_all.at[2, :, c_cols], x_all.at[2, :, c_cols], p_send.at[2, 0], p_recv.at[2, 0], mate)
+
+    def whole_start():
+        own_tokens.wait()
+        for k in range(3):
+            token_copy(k).wait_recv()
+        dispatch = picks[0, :, NA * 128 :] + picks[1, :, NA * 128 :]
+        for chip in range(4):
+            rows = lax.dot_general(
+                dispatch, tokens[chip], (((0,), (0,)), ((), ())), preferred_element_type=F32
+            ).astype(BF)
+            send_b[:, :, chip * FW : (chip + 1) * FW] = rows.reshape(E, SL, FW)
+        whole_own().start()
+        for k in range(NDP - 1):
+            go(whole_copy(k))
+
+    def whole_spread():
+        for k in range(NDP - 1):
+            whole_copy(k).wait_recv()
+        whole_own().wait()
+        go(whole_mate())
+
     def hidden_send(ch):
         return remote(hid.at[ch, 0], hid.at[ch, 1], h_send.at[ch], h_recv.at[ch], mate)
 
@@ -600,8 +677,8 @@
         u = jnp.dot(rows, wu_v[:, cols], preferred_element_type=F32)
         hid[ch, 0, :, cols] = (g / (1.0 + jnp.exp(-g)) * u).astype(BF)
 
-    def down(ch, owner):
-        cols = columns(owner)
+    def down(ch, chip):
+        cols = columns(chip)
         return jnp.dot(hid[ch, 0], wd_v[0, :, cols], preferred_element_type=F32) + jnp.dot(
             hid[ch, 1], wd_v[1, :, cols], preferred_element_type=F32
         )
@@ -636,7 +713,15 @@
             ).astype(BF)
             go(near(ch, side, side, hop_out.at[ch, side]))
 
-    ret_copies = []
+    e_of, j_of = dp // 2, lax.rem(dp, 2)
+
+    def back_copy(ch, k):
+        p = peers[k]
+        rows = pl.ds(pl.multiple_of(p * SL, SL), SL)
+        return remote(out.at[ch, rows], ret.at[ch, e_of, j_of], r_send.at[ch, k], r_recv.at[ch, k], {"dp": p})
+
+    def back_own(ch):
+        return pltpu.make_async_copy(out.at[ch, dp_rows], ret.at[ch, e_of, j_of], r_own.at[ch])
 
     def reduce_end(ch):
         for side in range(2):
@@ -644,78 +729,144 @@
                 near(ch, side, h, hop_out.at[ch, side]).wait_recv()
         total = own_part[ch] + fin[ch, 0].astype(F32) + fin[ch, 1].astype(F32)
         out[ch] = total.astype(BF)
-        own = pltpu.make_async_copy(
-            out.at[ch, pl.ds(pl.multiple_of(dp * SL, SL), SL)], ret.at[ch, dp], r_own.at[ch]
-        )
-        own.start()
-        cs = [own]
-        for k, p in enumerate(peers):
-            copy = remote(
-                out.at[ch, pl.ds(pl.multiple_of(p * SL, SL), SL)],
-                ret.at[ch, dp],
-                r_send.at[ch, k],
-                r_recv.at[ch, k],
-                {"dp": p},
-            )
-            copy.start()
-            cs.append(copy)
-        ret_copies.extend(cs)
+        back_own(ch).start()
+        for k in range(NDP - 1):
+            go(back_copy(ch, k))
+
+    def open_copy(k):
+        p = peers[k]
+        rows = pl.ds(pl.multiple_of(p * SL, SL), SL)
+        return remote(part_b.at[rows], ret_b.at[e_of, j_of], r_send.at[2, k], r_recv.at[2, k], {"dp": p})
+
+    def open_own():
+        return pltpu.make_async_copy(part_b.at[dp_rows], ret_b.at[e_of, j_of], r_own.at[2])
+
+    def open_start():
+        for chip in range(4):
+            part_b[:, chip * FW : (chip + 1) * FW] = down(2, chip).astype(BF)
+        open_own().start()
+        for k in range(NDP - 1):
+            go(open_copy(k))
+
+    def shares(k):
+        wide_w = jnp.broadcast_to(weight[k : k + 1, :], (128, 128)).T
+        return jnp.concatenate([wide_w] * (FW // 128), axis=1)
+
+    def moe_copy(k):
+        return remote(moe_out.at[k], moe_in.at[k], m_send.at[k], m_recv.at[k], x_peers[k])
+
+    def open_end():
+        for k in range(NDP - 1):
+            open_copy(k).wait_recv()
+        open_own().wait()
+        w = [shares(k) for k in range(2)]
+
+        def mix(chip):
+            both = [ret_b[:, j, :, columns(chip)].reshape(128, FW) for j in range(2)]
+            total = jnp.zeros((128, FW), F32)
+            for k in range(2):
+                pick = picks[k, :, NA * 128 :]
+                rows = jnp.dot(pick, both[0], preferred_element_type=F32)
+                rows = rows + jnp.dot(pick, both[1], preferred_element_type=F32)
+                total = total + w[k] * rows
+            return total
+
+        for k in (1, 0, 2):
+            moe_out[k] = mix(lax.rem(x + 1 + k, 4)).astype(BF)
+            go(moe_copy(k))
+        moe_own[...] = mix(x) + hidden[...]
+
+    def combine(ch):
+        for k in range(NDP - 1):
+            back_copy(ch, k).wait_recv()
+        back_own(ch).wait()
+        total = moe_own[...]
+        for k in range(2):
+            pick = picks[k, :, ch * 128 : (ch + 1) * 128]
+            rows = jnp.dot(pick, ret[ch, :, 0].reshape(128, FW), preferred_element_type=F32)
+            rows = rows + jnp.dot(pick, ret[ch, :, 1].reshape(128, FW), preferred_element_type=F32)
+            total = total + shares(k) * rows
+        moe_own[...] = total
 
     spread_own(0)
+    for copy in mate_w:
+        go(copy)
+    whole_start()
     spread_on(0)
     spread_own(1)
     spread_rest(0)
     spread_far(0)
-    for copy in w_copies[:2]:
+    for copy in w_copies[:16]:
         copy.wait()
+    spread_end(0)
+
+    gate_up(0, 0)
     spread_on(1)
-    spread_own(2)
-    spread_end(0)
-    for ch in range(NCH):
-        gate_up(ch, 0)
-        if ch == 0:
-            spread_rest(1)
-        if ch == 1:
-            reduce_hop(0)
-        if ch == 2:
-            reduce_hop(1)
-        gate_up(ch, 1)
-        if ch == 0:
-            spread_far(1)
-        if ch == 1:
-            spread_rest(2)
-        gate_up(ch, 2)
-        go(hidden_send(ch))
-        if ch == 0:
-            spread_on(2)
-            for copy in w_copies[2:]:
-                copy.wait()
-            for copy in mate_w:
-                copy.wait_recv()
-        if ch == 1:
-            spread_far(2)
-            reduce_end(0)
-        if ch == 2:
-            reduce_end(1)
-        hidden_send(ch).wait_recv()
-        reduce_start(ch)
-        reduce_own(ch)
-        if ch < 2:
-            spread_end(ch + 1)
-    reduce_hop(2)
-    reduce_end(2)
-    for copy in ret_copies:
+    gate_up(0, 1)
+    whole_spread()
+    gate_up(0, 2)
+    go(hidden_send(0))
+    spread_rest(1)
+    for copy in w_copies[16:]:
         copy.wait()
+    for copy in mate_w:
+        copy.wait_recv()
+    hidden_send(0).wait_recv()
+    reduce_start(0)
+    reduce_own(0)
+    spread_far(1)
+    whole_mate().wait_recv()
+
+    gate_up(2, 0)
+    gate_up(2, 1)
+    reduce_hop(0)
+    gate_up(2, 2)
+    go(hidden_send(2))
+    spread_end(1)
+    gate_up(1, 0)
+    hidden_send(2).wait_recv()
+    open_start()
+    gate_up(1, 1)
+    reduce_end(0)
+    gate_up(1, 2)
+    go(hidden_send(1))
+    hidden_send(1).wait_recv()
+    reduce_start(1)
+    reduce_own(1)
+    reduce_hop(1)
+    open_end()
+    combine(0)
+    reduce_end(1)
+    total = moe_own[...]
+    for k in range(3):
+        moe_copy(k).wait_recv()
+        total = total + moe_in[k].astype(F32)
+    moe_own[...] = total
+    combine(1)
+
+    mixed = moe_own[...]
+    squares[7] = square_sums(mixed)
+
+    def square_copy(k):
+        return remote(squares.at[7], squares.at[k], q_send.at[k], q_recv.at[k], {"mp": mp_peers[k]})
+
+    for k in range(7):
+        go(square_copy(k))
+    summed = squares[7]
+    for k in range(7):
+        square_copy(k).wait_recv()
+        summed = summed + squares[k]
+    result[...] = (mixed * as_columns(lax.rsqrt(summed / D + eps_norm)) * gain[...]).astype(BF)
     for copy in sent:
         copy.wait_send()
 
 
-def experts(send, wg, wu, wd, collective_id):
+def experts(send, normed, picks, weight, hidden, gain, wg, wu, wd, collective_id):
     anyspace = pl.BlockSpec(memory_space=pl.ANY)
     return pl.pallas_call(
         experts_kernel,
-        out_shape=jax.ShapeDtypeStruct((NCH, NDP, SL, FW), BF),
-        in_specs=vmem(1) + [anyspace] * 3,
+        out_shape=jax.ShapeDtypeStruct((128, FW), BF),
+        in_specs=vmem(6) + [anyspace] * 3,
         out_specs=vmem(1)[0],
         scratch_shapes=[
             pltpu.VMEM((NCH, RC, D), BF),
@@ -723,74 +874,52 @@
             pltpu.VMEM((D, HID), BF),
             pltpu.VMEM((2, HID, D // 2), BF),
             pltpu.VMEM((NCH, 2, RC, HID), BF),
-            pltpu.VMEM((NCH, 3, RC, FW), BF),
-            pltpu.VMEM((NCH, RC, FW), F32),
-            pltpu.VMEM((NCH, 2, RC // 2, FW), BF),
-            pltpu.VMEM((NCH, 2, RC // 2, FW), BF),
-            pltpu.VMEM((NCH, 2, RC, FW), BF),
-            pltpu.VMEM((NCH, RC, FW), BF),
-            DMA((6,)),
+            pltpu.VMEM((NA, 3, RC, FW), BF),
+            pltpu.VMEM((NA, RC, FW), F32),
+            pltpu.VMEM((NA, 2, RC // 2, FW), BF),
+            pltpu.VMEM((NA, 2, RC // 2, FW), BF),
+            pltpu.VMEM((NA, 2, RC, FW), BF),
+            pltpu.VMEM((NA, RC, FW), BF),
+            pltpu.VMEM((NA, E, 2, SL, FW), BF),
+            pltpu.VMEM((4, 128, FW), BF),
+            pltpu.VMEM((E, SL, 4 * FW), BF),
+            pltpu.VMEM((RC, 4 * FW), BF),
+            pltpu.VMEM((E, 2, SL, 4 * FW), BF),
+            pltpu.VMEM((3, 128, FW), BF),
+            pltpu.VMEM((3, 128, FW), BF),
+            pltpu.VMEM((128, FW), F32),
+            pltpu.VMEM((8, 8, 128), F32),
+            DMA((20,)),
             DMA((4,)),
             DMA((4,)),
             DMA((NCH, NDP - 1)),
             DMA((NCH, NDP - 1)),
-            DMA((NCH,)),
-            DMA((NCH, 2, 2)),
-            DMA((NCH, 2, 2)),
-            DMA((NCH, 2)),
-            DMA((NCH, 2)),
+            DMA((4,)),
+            DMA((NA, 2, 2)),
+            DMA((NA, 2, 2)),
+            DMA((NA, 2)),
+            DMA((NA, 2)),
             DMA((NCH, 4)),
             DMA((NCH, 4)),
             DMA((NCH,)),
             DMA((NCH,)),
-            DMA((NCH, 2)),
-            DMA((NCH, 2)),
-            DMA((NCH, 2, 2)),
-            DMA((NCH, 2, 2)),
+            DMA((NA, 2)),
+            DMA((NA, 2)),
+            DMA((NA, 2, 2)),
+            DMA((NA, 2, 2)),
             DMA((NCH, NDP - 1)),
             DMA((NCH, NDP - 1)),
             DMA((NCH,)),
+            DMA((3,)),
+            DMA((3,)),
+            DMA((3,)),
+            DMA((3,)),
+            DMA((7,)),
+            DMA((7,)),
         ],
         compiler_params=comm_params(collective_id),
         name="experts",
-    )(send, wg, wu, wd)
-
-
-def closing_kernel(ret, picks, weight, hidden, gain, out, squares, send, recv):
-    me = lax.axis_index("mp")
-    peers = [lax.rem(me + k, 8) for k in range(1, 8)]
-    greet([{"mp": p} for p in peers])
-    mixed = hidden[...]
-    for k in range(2):
-        rows = jnp.zeros((128, FW), F32)
-        for j in range(2):
-            back = ret[:, j].reshape(E * C, FW)
-            rows = rows + jnp.dot(picks[k], back, preferred_element_type=F32)
-        mixed = mixed + weight[:, k : k + 1] * rows
-    squares[7] = square_sums(mixed)
-    copies = []
-    for k, p in enumerate(peers):
-        copies.append(remote(squares.at[7], squares.at[k], send.at[k], recv.at[k], {"mp": p}))
-        copies[-1].start()
-    summed = squares[7]
-    for k, copy in enumerate(copies):
-        copy.wait_recv()
-        summed = summed + squares[k]
-    out[...] = (mixed * as_columns(lax.rsqrt(summed / D + eps_norm)) * gain[...]).astype(BF)
-    for copy in copies:
-        copy.wait_send()
-
-
-def closing_norm(ret, picks, weight, hidden, gain, collective_id):
-    return pl.pallas_call(
-        closing_kernel,
-        out_shape=jax.ShapeDtypeStruct((128, FW), BF),
-        in_specs=vmem(5),
-        out_specs=vmem(1)[0],
-        scratch_shapes=[pltpu.VMEM((8, 8, 128), F32), DMA((7,)), DMA((7,))],
-        compiler_params=comm_params(collective_id),
-        name="closing_norm",
-    )(ret, picks, weight, hidden, gain)
+    )(send, normed, picks, weight, hidden, gain, wg, wu, wd)
 
 
 def local(
@@ -811,9 +940,7 @@
     down_proj,
     final_gain,
 ):
-    column_start = lax.axis_index("mp") * FW
-    gain_cols = lax.dynamic_slice_in_dim(attn_gain, column_start, FW, 0)
-    send, hidden, picks = attend(
+    send, normed, hidden, picks = attend(
         queries,
         new_keys,
         new_values,
@@ -823,13 +950,21 @@
         page_order.reshape(16, 128),
         out_proj,
         residual,
-        gain_cols[None, :],
-        routes,
+        attn_gain.reshape(32, 128),
+        routes.T,
         0,
     )
-    returned = experts(send, gate_proj, up_proj, down_proj, 1)
-    return closing_norm(
-        returned.reshape(NCH * E, 2, SL, FW), picks, route_weight, hidden, final_gain[None, :], 2
+    return experts(
+        send,
+        normed,
+        picks,
+        route_weight.T,
+        hidden,
+        final_gain[None, :],
+        gate_proj,
+        up_proj,
+        down_proj,
+        1,
     )
 
 

time: 143 us -> 127 us (0.89)
  Pallas kernels: 137 us -> 125 us
  local copies, waits for them, and re-layouts: 5.05 us -> 1.57 us
    pallas_call x3 -> x2, Pallas kernels: 137 us -> 125 us  [the longest x1 74.6 us: experts(): pl.pallas_call(experts_kernel, out_shape=jax.ShapeDtypeStruct((128, FW),...]
    unnamed x5 -> x1, local copies, waits for them, and re-layouts: 3.73 us -> 1.57 us
where the time goes in v3:
time: 127 us; the launch traced here: 126 us
  Pallas kernels  125 us (98%)
  local copies, waits for them, and re-layouts  1.57 us (1%)
    pallas_call x1, Pallas kernels, experts(): pl.pallas_call(experts_kernel, out_shape=jax.ShapeDtypeStruct((128, FW),...  74.6 us
    pallas_call x1, Pallas kernels, attend(): pl.pallas_call(attend_kernel, out_shape=(jax.ShapeDtypeStruct((NA, E, SL,...  50.1 us

profile of v3, /device:TPU:1, one launch (start us, length us, event | category | flops | bytes accessed | tf_op | source)
XLA Modules:
  0.0 126.3 jit_solution(13796971829075707888)
XLA Ops:
  0.0 50.1 %attend.1 = (bf16[2,8,16,512]{3,2,1,0:T(8,128)(2,1)}, bf16[128,512]{1,0:T(8,128)(2,1)}, f32[128,512]{1,0:T(8,128)}, bf16[2,128,384]{2,1,0:T(8,128)(2,1)}) custom-call(bf16[128,512]{1,0:T(8,128)(2,1)} %queries.1, bf16[128,128]{1,0:T(8,128)(2,1)} %new_keys.1, bf16[128,128]{1,0:T(8,128)(2,1)} %new_values.1, bf16[2048,128]{1,0:T(8,128)(2,1)} %bitcast.8, ...), custom_call_target="tpu_custom_call" | custom-call | tf_op jit(solution)/shard_map/attend/pallas_call | solution.py:403
  50.1 74.6 %experts.1 = bf16[128,512]{1,0:T(8,128)(2,1)} custom-call(bf16[2,8,16,512]{3,2,1,0:T(8,128)(2,1)} %get-tuple-element.9.send, bf16[128,512]{1,0:T(8,128)(2,1)} %get-tuple-element.10.normed, bf16[2,128,384]{2,1,0:T(8,128)(2,1)} %get-tuple-element.11.picks, f32[2,128]{1,0:T(2,128)} %bitcast.15, f32[128,512]{1,0:T(8,128)} %get-tuple-element.12.hidden, ...), custom_call_target="tpu_custom_call" | custom-call | tf_op jit(solution)/shard_map/experts/pallas_call | solution.py:866
  124.8 1.6 %copy.18 = bf16[128,512]{1,0:T(8,128)(2,1)} copy(bf16[128,512]{1,0:T(8,128)(2,1)} %experts.1) | data formatting | bytes 262144

commit v4 on v3

--- a/solution.py
+++ b/solution.py
@@ -58,10 +58,6 @@
     )
 
 
-def vmem(count):
-    return [pl.BlockSpec(memory_space=pltpu.VMEM)] * count
-
-
 def iota(shape, axis):
     return lax.broadcasted_iota(jnp.int32, shape, axis)
 
@@ -86,7 +82,7 @@
     return stack.T
 
 
-def attend_kernel(
+def layer_kernel(
     queries,
     new_keys,
     new_values,
@@ -96,12 +92,14 @@
     order,
     out_proj,
     residual,
-    gain,
+    attn_gain,
     routes,
-    send,
-    normed_out,
-    hidden,
-    picks,
+    weight,
+    final_gain,
+    wg,
+    wu,
+    wd,
+    result,
     q_all,
     keys_v,
     values_v,
@@ -116,9 +114,31 @@
     stat_out,
     stat_in,
     attn,
-    part,
+    proj_part,
     got,
     squares,
+    hidden,
+    picks,
+    send,
+    x_all,
+    wg_v,
+    wu_v,
+    wd_v,
+    hid,
+    part,
+    own_part,
+    hop_in,
+    hop_out,
+    fin,
+    out,
+    ret,
+    tokens,
+    send_b,
+    part_b,
+    ret_b,
+    moe_out,
+    moe_in,
+    moe_own,
     l_sems,
     s1,
     r1,
@@ -130,15 +150,77 @@
     tr,
     ps,
     pr,
-    qs,
-    qr,
+    w_sems,
+    a_own,
+    r_own,
+    wp_send,
+    wp_recv,
+    a_send,
+    a_recv,
+    g_send,
+    g_recv,
+    f_send,
+    f_recv,
+    p_send,
+    p_recv,
+    h_send,
+    h_recv,
+    t_send,
+    t_recv,
+    n_send,
+    n_recv,
+    r_send,
+    r_recv,
+    k_send,
+    k_recv,
+    m_send,
+    m_recv,
+    q_send,
+    q_recv,
 ):
     dp = lax.axis_index("dp")
     mp = lax.axis_index("mp")
     z, y = dp // 4, lax.rem(dp, 4)
     scale = HD ** (-0.5)
-    dp_peers = [lax.rem(dp + k, NDP) for k in range(1, NDP)]
+    peers = [lax.rem(dp + k, NDP) for k in range(1, NDP)]
     mp_peers = [lax.rem(mp + k, 8) for k in range(1, 8)]
+    x, c = mp // 2, lax.rem(mp, 2)
+    xr, xo, xl = lax.rem(x + 1, 4), lax.rem(x + 2, 4), lax.rem(x + 3, 4)
+    mr, mo, ml = xr * 2 + c, xo * 2 + c, xl * 2 + c
+    right, left, mate = {"mp": mr}, {"mp": ml}, {"mp": x * 2 + 1 - c}
+    sides = (right, left)
+    x_peers = [{"mp": lax.rem(x + k, 4) * 2 + c} for k in range(1, 4)]
+    half = RC // 2
+
+    def wide(owner):
+        return pl.ds(pl.multiple_of((lax.rem(owner, 2) * 4 + owner // 2) * FW, FW), FW)
+
+    def columns(owner):
+        return pl.ds(pl.multiple_of(owner * FW, FW), FW)
+
+    dp_rows = pl.ds(pl.multiple_of(dp * SL, SL), SL)
+    c_cols = pl.ds(pl.multiple_of(c * 4 * FW, 4 * FW), 4 * FW)
+    mate_cols = pl.ds(pl.multiple_of((1 - c) * 4 * FW, 4 * FW), 4 * FW)
+
+    w_copies = []
+    for w, (src, dst) in enumerate(((wg, wg_v), (wu, wu_v))):
+        for core in range(2):
+            for chip in range(4):
+                w_copies.append(
+                    pltpu.make_async_copy(
+                        src.at[pl.ds((chip * 2 + core) * FW, FW), :],
+                        dst.at[pl.ds((core * 4 + chip) * FW, FW), :],
+                        w_sems.at[w * 8 + core * 4 + chip],
+                    )
+                )
+    for j in range(4):
+        w_copies.append(
+            pltpu.make_async_copy(
+                wd.at[:, pl.ds(pl.multiple_of(j * 1024 + c * FW, FW), FW)],
+                wd_v.at[0, :, pl.ds(j * FW, FW)],
+                w_sems.at[16 + j],
+            )
+        )
     loads = [
         pltpu.make_async_copy(keys, keys_v, l_sems.at[0]),
         pltpu.make_async_copy(values, values_v, l_sems.at[1]),
@@ -159,7 +241,9 @@
     loads[0].start()
     loads[1].start()
     own_q.wait()
-    greet([{"dp": p} for p in dp_peers] + [{"mp": p} for p in mp_peers])
+    for copy in w_copies:
+        copy.start()
+    greet([{"dp": p} for p in peers] + [{"mp": p} for p in mp_peers])
     sent = []
 
     def go(copy):
@@ -186,6 +270,18 @@
     for h in range(2):
         for k in range(1, 4):
             go(second(h, 0, k))
+    mate_w = []
+    for j in range(4):
+        mate_w.append(
+            remote(
+                wd.at[:, pl.ds(pl.multiple_of(j * 1024 + (1 - c) * FW, FW), FW)],
+                wd_v.at[1, :, pl.ds(j * FW, FW)],
+                wp_send.at[j],
+                wp_recv.at[j],
+                mate,
+            )
+        )
+        go(mate_w[j])
 
     lane = iota((128, 128), 1)
     row = iota((128, 128), 0)
@@ -208,7 +304,7 @@
 
     for k in range(1, 4):
         for h in range(2):
-            remote(q_half(dp, h), q_half(group(h, -k, 0), h), s1.at[h, k - 1], r1.at[h, k - 1], {"dp": dp_peers[0]}).wait_recv()
+            remote(q_half(dp, h), q_half(group(h, -k, 0), h), s1.at[h, k - 1], r1.at[h, k - 1], {"dp": peers[0]}).wait_recv()
             for kk in range(1, 4):
                 go(second(h, k, kk))
 
@@ -259,8 +355,8 @@
         a = attn[rows, :]
         for k, p in enumerate(mp_peers):
             cols = pl.ds(pl.multiple_of(p * FW, FW), FW)
-            part[t, k] = jnp.dot(a, proj_v[:, cols], preferred_element_type=F32).astype(BF)
-            go(remote(part.at[t, k], got.at[t, k], ps.at[t, k], pr.at[t, k], {"mp": p}))
+            proj_part[t, k] = jnp.dot(a, proj_v[:, cols], preferred_element_type=F32).astype(BF)
+            go(remote(proj_part.at[t, k], got.at[t, k], ps.at[t, k], pr.at[t, k], {"mp": p}))
         cols = pl.ds(pl.multiple_of(mp * FW, FW), FW)
         own = jnp.dot(a, proj_v[:, cols], preferred_element_type=F32)
         hidden[rows, :] = own + residual[rows, :].astype(F32)
@@ -269,7 +365,7 @@
         rows = slice(t * 64, (t + 1) * 64)
         total = hidden[rows, :]
         for k in range(7):
-            remote(part.at[t, k], got.at[t, k], ps.at[t, k], pr.at[t, k], {"mp": mp_peers[k]}).wait_recv()
+            remote(proj_part.at[t, k], got.at[t, k], ps.at[t, k], pr.at[t, k], {"mp": mp_peers[k]}).wait_recv()
             total = total + got[t, k].astype(F32)
         hidden[rows, :] = total
 
@@ -286,7 +382,7 @@
         for k in range(1, 4):
             for h in range(2):
                 remote(
-                    q_half(dp, h), q_half(group(h, -j, -k), h), s2.at[h, j, k - 1], r2.at[h, j, k - 1], {"dp": dp_peers[0]}
+                    q_half(dp, h), q_half(group(h, -j, -k), h), s2.at[h, j, k - 1], r2.at[h, j, k - 1], {"dp": peers[0]}
                 ).wait_recv()
 
     page_q[...] = jnp.dot(owners[...], q_all[...], preferred_element_type=F32)
@@ -338,18 +434,48 @@
         return val_out.at[pl.ds(pl.multiple_of(p * DEC, DEC), DEC), :]
 
     def swap_stat(k):
-        p = dp_peers[k]
+        p = peers[k]
         return remote(stat_out.at[p // 2], stat_in.at[k], ts.at[k], tr.at[k], {"dp": p})
 
     def swap_val(k):
-        p = dp_peers[k]
+        p = peers[k]
         return remote(val_rows(p), val_in.at[k], vs.at[k], vr.at[k], {"dp": p})
 
     for k in range(NDP - 1):
         go(swap_stat(k))
         go(swap_val(k))
 
+    def square_copy(t, k):
+        return remote(squares.at[t, 7], squares.at[t, k], q_send.at[t, k], q_recv.at[t, k], {"mp": mp_peers[k]})
+
+    def row_scales(t, rows):
+        squares[t, 7] = square_sums(rows)
+        for k in range(7):
+            go(square_copy(t, k))
+        summed = squares[t, 7]
+        for k in range(7):
+            square_copy(t, k).wait_recv()
+            summed = summed + squares[t, k]
+        return as_columns(lax.rsqrt(summed / D + eps_norm))
+
+    def token_copy(t, k):
+        rows = tokens.at[x, pl.ds(t * 64, 64), :]
+        return remote(rows, rows, k_send.at[t, k], k_recv.at[t, k], x_peers[k])
+
+    gain_rows = attn_gain[pl.ds(mp * 4, 4), :]
+    gain_cols = jnp.concatenate([gain_rows[i : i + 1, :] for i in range(4)], axis=1)
+    nothing = jnp.zeros((64, FW), F32)
+
+    def finish(t):
+        mine = hidden[t * 64 : (t + 1) * 64, :]
+        scales = row_scales(t, jnp.concatenate([nothing, mine] if t else [mine, nothing], axis=0))
+        scales = scales[t * 64 : (t + 1) * 64, :]
+        tokens[x, t * 64 : (t + 1) * 64, :] = (mine * scales * gain_cols).astype(BF)
+        for k in (0, 2, 1):
+            go(token_copy(t, k))
+
     collect(1)
+    finish(1)
     for k in range(NDP - 1):
         swap_stat(k).wait_recv()
     stat_in[NDP - 1] = stat_out[dp // 2]
@@ -377,218 +503,7 @@
     project(0)
     collect(0)
 
-    squares[7] = square_sums(hidden[...])
-    for k, p in enumerate(mp_peers):
-        go(remote(squares.at[7], squares.at[k], qs.at[k], qr.at[k], {"mp": p}))
-    summed = squares[7]
-    for k, p in enumerate(mp_peers):
-        remote(squares.at[7], squares.at[k], qs.at[k], qr.at[k], {"mp": p}).wait_recv()
-        summed = summed + squares[k]
-    gain_rows = gain[pl.ds(mp * 4, 4), :]
-    gain_cols = jnp.concatenate([gain_rows[i : i + 1, :] for i in range(4)], axis=1)
-    normed = (hidden[...] * as_columns(lax.rsqrt(summed / D + eps_norm)) * gain_cols).astype(BF)
-    normed_out[...] = normed
-    dispatch = picks[0] + picks[1]
-    for ch in range(NA):
-        rows = lax.dot_general(
-            dispatch[:, ch * 128 : (ch + 1) * 128], normed, (((0,), (0,)), ((), ())), preferred_element_type=F32
-        ).astype(BF)
-        send[ch] = rows.reshape(E, SL, FW)
-    for copy in sent:
-        copy.wait_send()
-
-
-def attend(queries, new_keys, new_values, keys, values, lengths, order, out_proj, residual, gain, routes, collective_id):
-    anyspace = pl.BlockSpec(memory_space=pl.ANY)
-    return pl.pallas_call(
-        attend_kernel,
-        out_shape=(
-            jax.ShapeDtypeStruct((NA, E, SL, FW), BF),
-            jax.ShapeDtypeStruct((128, FW), BF),
-            jax.ShapeDtypeStruct((128, FW), F32),
-            jax.ShapeDtypeStruct((2, 128, E * C), BF),
-        ),
-        in_specs=vmem(3) + [anyspace] * 2 + vmem(2) + [anyspace] + vmem(3),
-        out_specs=tuple(vmem(4)),
-        scratch_shapes=[
-            pltpu.VMEM((NDP * DEC, FW), BF),
-            pltpu.VMEM((2048, HD), BF),
-            pltpu.VMEM((2048, HD), BF),
-            pltpu.VMEM((FW, D), BF),
-            pltpu.VMEM((128, NDP * DEC), BF),
-            pltpu.VMEM((4, 128, 128), F32),
-            pltpu.VMEM((4, 128, 128), F32),
-            pltpu.VMEM((128, FW), F32),
-            pltpu.VMEM((128, FW), BF),
-            pltpu.VMEM((NDP * DEC, FW), BF),
-            pltpu.VMEM((NDP - 1, DEC, FW), BF),
-            pltpu.VMEM((8, 8, 128), F32),
-            pltpu.VMEM((NDP, 8, 128), F32),
-            pltpu.VMEM((128, FW), BF),
-            pltpu.VMEM((2, 7, 64, FW), BF),
-            pltpu.VMEM((2, 7, 64, FW), BF),
-            pltpu.VMEM((8, 8, 128), F32),
-            DMA((4,)),
-            DMA((2, 3)),
-            DMA((2, 3)),
-            DMA((2, 4, 3)),
-            DMA((2, 4, 3)),
-            DMA((NDP - 1,)),
-            DMA((NDP - 1,)),
-            DMA((NDP - 1,)),
-            DMA((NDP - 1,)),
-            DMA((2, 7)),
-            DMA((2, 7)),
-            DMA((7,)),
-            DMA((7,)),
-        ],
-        compiler_params=comm_params(collective_id),
-        name="attend",
-    )(queries, new_keys, new_values, keys, values, lengths, order, out_proj, residual, gain, routes)
-
-
-def experts_kernel(
-    send,
-    normed,
-    picks,
-    weight,
-    hidden,
-    gain,
-    wg,
-    wu,
-    wd,
-    result,
-    x_all,
-    wg_v,
-    wu_v,
-    wd_v,
-    hid,
-    part,
-    own_part,
-    hop_in,
-    hop_out,
-    fin,
-    out,
-    ret,
-    tokens,
-    send_b,
-    part_b,
-    ret_b,
-    moe_out,
-    moe_in,
-    moe_own,
-    squares,
-    w_sems,
-    wp_send,
-    wp_recv,
-    a_send,
-    a_recv,
-    a_own,
-    g_send,
-    g_recv,
-    f_send,
-    f_recv,
-    p_send,
-    p_recv,
-    h_send,
-    h_recv,
-    t_send,
-    t_recv,
-    n_send,
-    n_recv,
-    r_send,
-    r_recv,
-    r_own,
-    k_send,
-    k_recv,
-    m_send,
-    m_recv,
-    q_send,
-    q_recv,
-):
-    dp = lax.axis_index("dp")
-    mp = lax.axis_index("mp")
-    x, c = mp // 2, lax.rem(mp, 2)
-    xr, xo, xl = lax.rem(x + 1, 4), lax.rem(x + 2, 4), lax.rem(x + 3, 4)
-    mr, mo, ml = xr * 2 + c, xo * 2 + c, xl * 2 + c
-    right, left, mate = {"mp": mr}, {"mp": ml}, {"mp": x * 2 + 1 - c}
-    sides = (right, left)
-    peers = [lax.rem(dp + k, NDP) for k in range(1, NDP)]
-    mp_peers = [lax.rem(mp + k, 8) for k in range(1, 8)]
-    x_peers = [{"mp": lax.rem(x + k, 4) * 2 + c} for k in range(1, 4)]
-    half = RC // 2
-
-    def wide(owner):
-        return pl.ds(pl.multiple_of((lax.rem(owner, 2) * 4 + owner // 2) * FW, FW), FW)
-
-    def columns(owner):
-        return pl.ds(pl.multiple_of(owner * FW, FW), FW)
-
-    dp_rows = pl.ds(pl.multiple_of(dp * SL, SL), SL)
-    c_cols = pl.ds(pl.multiple_of(c * 4 * FW, 4 * FW), 4 * FW)
-    mate_cols = pl.ds(pl.multiple_of((1 - c) * 4 * FW, 4 * FW), 4 * FW)
-
-    w_copies = []
-    for w, (src, dst) in enumerate(((wg, wg_v), (wu, wu_v))):
-        for core in range(2):
-            for chip in range(4):
-                w_copies.append(
-                    pltpu.make_async_copy(
-                        src.at[pl.ds((chip * 2 + core) * FW, FW), :],
-                        dst.at[pl.ds((core * 4 + chip) * FW, FW), :],
-                        w_sems.at[w * 8 + core * 4 + chip],
-                    )
-                )
-    for j in range(4):
-        w_copies.append(
-            pltpu.make_async_copy(
-                wd.at[:, pl.ds(pl.multiple_of(j * 1024 + c * FW, FW), FW)],
-                wd_v.at[0, :, pl.ds(j * FW, FW)],
-                w_sems.at[16 + j],
-            )
-        )
-    own_tokens = pltpu.make_async_copy(normed, tokens.at[x], a_own.at[3])
-    own_tokens.start()
-    greet([{"dp": p} for p in peers] + [{"mp": p} for p in mp_peers])
-
-    sent = []
-
-    def go(copy):
-        copy.start()
-        sent.append(copy)
-
-    def token_copy(k):
-        return remote(normed, tokens.at[x], k_send.at[k], k_recv.at[k], x_peers[k])
-
-    for k in (0, 2, 1):
-        go(token_copy(k))
-
-    out_copies, own_copies = [], []
-    for ch in range(NA):
-        own = pltpu.make_async_copy(send.at[ch, dp // 2], x_all.at[ch, dp_rows, wide(mp)], a_own.at[ch])
-        own.start()
-        own_copies.append(own)
-        cs = []
-        for k, p in enumerate(peers):
-            copy = remote(
-                send.at[ch, p // 2], x_all.at[ch, dp_rows, wide(mp)], a_send.at[ch, k], a_recv.at[ch, k], {"dp": p}
-            )
-            go(copy)
-            cs.append(copy)
-        out_copies.append(cs)
-    for copy in w_copies:
-        copy.start()
-    mate_w = []
-    for j in range(4):
-        mate_w.append(
-            remote(
-                wd.at[:, pl.ds(pl.multiple_of(j * 1024 + (1 - c) * FW, FW), FW)],
-                wd_v.at[1, :, pl.ds(j * FW, FW)],
-                wp_send.at[j],
-                wp_recv.at[j],
-                mate,
-            )
-        )
+    finish(0)
 
     def block(ch, h, owner):
         return x_all.at[ch, pl.ds(h * half, half), wide(owner)]
@@ -609,10 +524,19 @@
         owner = (mp, ml, mr, mo)[which]
         return remote(whole(ch, owner), whole(ch, owner), p_send.at[ch, which], p_recv.at[ch, which], mate)
 
+    def slice_copy(ch, k):
+        p = peers[k]
+        return remote(
+            send.at[ch, p // 2], x_all.at[ch, dp_rows, wide(mp)], a_send.at[ch, k], a_recv.at[ch, k], {"dp": p}
+        )
+
+    def slice_own(ch):
+        return pltpu.make_async_copy(send.at[ch, dp // 2], x_all.at[ch, dp_rows, wide(mp)], a_own.at[ch])
+
     def spread_own(ch):
-        for copy in out_copies[ch]:
-            copy.wait_recv()
-        own_copies[ch].wait()
+        for k in range(NDP - 1):
+            slice_copy(ch, k).wait_recv()
+        slice_own(ch).wait()
         for h in range(2):
             go(neighbour(ch, 0, h))
             go(neighbour(ch, 1, 1 - h))
@@ -648,9 +572,9 @@
         return remote(x_all.at[2, :, c_cols], x_all.at[2, :, c_cols], p_send.at[2, 0], p_recv.at[2, 0], mate)
 
     def whole_start():
-        own_tokens.wait()
-        for k in range(3):
-            token_copy(k).wait_recv()
+        for t in range(2):
+            for k in range(3):
+                token_copy(t, k).wait_recv()
         dispatch = picks[0, :, NA * 128 :] + picks[1, :, NA * 128 :]
         for chip in range(4):
             rows = lax.dot_general(
@@ -788,9 +712,16 @@
             total = total + shares(k) * rows
         moe_own[...] = total
 
+    dispatch = picks[0] + picks[1]
+    for ch in range(NA):
+        rows = lax.dot_general(
+            dispatch[:, ch * 128 : (ch + 1) * 128], tokens[x], (((0,), (0,)), ((), ())), preferred_element_type=F32
+        ).astype(BF)
+        send[ch] = rows.reshape(E, SL, FW)
+        slice_own(ch).start()
+        for k in range(NDP - 1):
+            go(slice_copy(ch, k))
     spread_own(0)
-    for copy in mate_w:
-        go(copy)
     whole_start()
     spread_on(0)
     spread_own(1)
@@ -845,56 +776,79 @@
     combine(1)
 
     mixed = moe_own[...]
-    squares[7] = square_sums(mixed)
-
-    def square_copy(k):
-        return remote(squares.at[7], squares.at[k], q_send.at[k], q_recv.at[k], {"mp": mp_peers[k]})
-
-    for k in range(7):
-        go(square_copy(k))
-    summed = squares[7]
-    for k in range(7):
-        square_copy(k).wait_recv()
-        summed = summed + squares[k]
-    result[...] = (mixed * as_columns(lax.rsqrt(summed / D + eps_norm)) * gain[...]).astype(BF)
+    result[...] = (mixed * row_scales(2, mixed) * final_gain[...]).astype(BF)
     for copy in sent:
         copy.wait_send()
 
 
-def experts(send, normed, picks, weight, hidden, gain, wg, wu, wd, collective_id):
-    anyspace = pl.BlockSpec(memory_space=pl.ANY)
+V = pltpu.VMEM
+
+
+def layer(operands, collective_id):
+    spaces = [pltpu.VMEM] * 3 + [pl.ANY] * 2 + [pltpu.VMEM] * 2 + [pl.ANY] + [pltpu.VMEM] * 5 + [pl.ANY] * 3
     return pl.pallas_call(
-        experts_kernel,
+        layer_kernel,
         out_shape=jax.ShapeDtypeStruct((128, FW), BF),
-        in_specs=vmem(6) + [anyspace] * 3,
-        out_specs=vmem(1)[0],
+        in_specs=[pl.BlockSpec(memory_space=space) for space in spaces],
+        out_specs=pl.BlockSpec(memory_space=pltpu.VMEM),
         scratch_shapes=[
-            pltpu.VMEM((NCH, RC, D), BF),
-            pltpu.VMEM((D, HID), BF),
-            pltpu.VMEM((D, HID), BF),
-            pltpu.VMEM((2, HID, D // 2), BF),
-            pltpu.VMEM((NCH, 2, RC, HID), BF),
-            pltpu.VMEM((NA, 3, RC, FW), BF),
-            pltpu.VMEM((NA, RC, FW), F32),
-            pltpu.VMEM((NA, 2, RC // 2, FW), BF),
-            pltpu.VMEM((NA, 2, RC // 2, FW), BF),
-            pltpu.VMEM((NA, 2, RC, FW), BF),
-            pltpu.VMEM((NA, RC, FW), BF),
-            pltpu.VMEM((NA, E, 2, SL, FW), BF),
-            pltpu.VMEM((4, 128, FW), BF),
-            pltpu.VMEM((E, SL, 4 * FW), BF),
-            pltpu.VMEM((RC, 4 * FW), BF),
-            pltpu.VMEM((E, 2, SL, 4 * FW), BF),
-            pltpu.VMEM((3, 128, FW), BF),
-            pltpu.VMEM((3, 128, FW), BF),
-            pltpu.VMEM((128, FW), F32),
-            pltpu.VMEM((8, 8, 128), F32),
+            V((NDP * DEC, FW), BF),
+            V((2048, HD), BF),
+            V((2048, HD), BF),
+            V((FW, D), BF),
+            V((128, NDP * DEC), BF),
+            V((4, 128, 128), F32),
+            V((4, 128, 128), F32),
+            V((128, FW), F32),
+            V((128, FW), BF),
+            V((NDP * DEC, FW), BF),
+            V((NDP - 1, DEC, FW), BF),
+            V((8, 8, 128), F32),
+            V((NDP, 8, 128), F32),
+            V((128, FW), BF),
+            V((2, 7, 64, FW), BF),
+            V((2, 7, 64, FW), BF),
+            V((3, 8, 8, 128), F32),
+            V((128, FW), F32),
+            V((2, 128, E * C), BF),
+            V((NA, E, SL, FW), BF),
+            V((NCH, RC, D), BF),
+            V((D, HID), BF),
+            V((D, HID), BF),
+            V((2, HID, D // 2), BF),
+            V((NCH, 2, RC, HID), BF),
+            V((NA, 3, RC, FW), BF),
+            V((NA, RC, FW), F32),
+            V((NA, 2, RC // 2, FW), BF),
+            V((NA, 2, RC // 2, FW), BF),
+            V((NA, 2, RC, FW), BF),
+            V((NA, RC, FW), BF),
+            V((NA, E, 2, SL, FW), BF),
+            V((4, 128, FW), BF),
+            V((E, SL, 4 * FW), BF),
+            V((RC, 4 * FW), BF),
+            V((E, 2, SL, 4 * FW), BF),
+            V((3, 128, FW), BF),
+            V((3, 128, FW), BF),
+            V((128, FW), F32),
+            DMA((4,)),
+            DMA((2, 3)),
+            DMA((2, 3)),
+            DMA((2, 4, 3)),
+            DMA((2, 4, 3)),
+            DMA((NDP - 1,)),
+            DMA((NDP - 1,)),
+            DMA((NDP - 1,)),
+            DMA((NDP - 1,)),
+            DMA((2, 7)),
+            DMA((2, 7)),
             DMA((20,)),
+            DMA((3,)),
+            DMA((NCH,)),
             DMA((4,)),
             DMA((4,)),
             DMA((NCH, NDP - 1)),
             DMA((NCH, NDP - 1)),
-            DMA((4,)),
             DMA((NA, 2, 2)),
             DMA((NA, 2, 2)),
             DMA((NA, 2)),
@@ -909,17 +863,16 @@
             DMA((NA, 2, 2)),
             DMA((NCH, NDP - 1)),
             DMA((NCH, NDP - 1)),
-            DMA((NCH,)),
+            DMA((2, 3)),
+            DMA((2, 3)),
             DMA((3,)),
             DMA((3,)),
-            DMA((3,)),
-            DMA((3,)),
-            DMA((7,)),
-            DMA((7,)),
+            DMA((3, 7)),
+            DMA((3, 7)),
         ],
         compiler_params=comm_params(collective_id),
-        name="experts",
-    )(send, normed, picks, weight, hidden, gain, wg, wu, wd)
+        name="layer",
+    )(*operands)
 
 
 def local(
@@ -940,31 +893,26 @@
     down_proj,
     final_gain,
 ):
-    send, normed, hidden, picks = attend(
-        queries,
-        new_keys,
-        new_values,
-        cache_keys.reshape(-1, HD),
-        cache_values.reshape(-1, HD),
-        cache_len.reshape(8, 128),
-        page_order.reshape(16, 128),
-        out_proj,
-        residual,
-        attn_gain.reshape(32, 128),
-        routes.T,
+    return layer(
+        (
+            queries,
+            new_keys,
+            new_values,
+            cache_keys.reshape(-1, HD),
+            cache_values.reshape(-1, HD),
+            cache_len.reshape(8, 128),
+            page_order.reshape(16, 128),
+            out_proj,
+            residual,
+            attn_gain.reshape(32, 128),
+            routes.T,
+            route_weight.T,
+            final_gain[None, :],
+            gate_proj,
+            up_proj,
+            down_proj,
+        ),
         0,
-    )
-    return experts(
-        send,
-        normed,
-        picks,
-        route_weight.T,
-        hidden,
-        final_gain[None, :],
-        gate_proj,
-        up_proj,
-        down_proj,
-        1,
     )
 
 

time: 127 us -> 121 us (0.953)
  Pallas kernels: 125 us -> 119 us
    pallas_call x2 -> x1, Pallas kernels: 125 us -> 119 us  [layer(): pl.pallas_call(layer_kernel, out_shape=jax.ShapeDtypeStruct((128, FW), BF...]
where the time goes in v4:
time: 121 us
  Pallas kernels  119 us (98%)
  local copies, waits for them, and re-layouts  1.57 us (1%)
    pallas_call x1, Pallas kernels, layer(): pl.pallas_call(layer_kernel, out_shape=jax.ShapeDtypeStruct((128, FW), BF...  119 us

profile of v4, /device:TPU:1, one launch (start us, length us, event | category | flops | bytes accessed | tf_op | source)
XLA Modules:
  0.0 121.0 jit_solution(813109673103430673)
XLA Ops:
  0.0 119.5 %layer.1 = bf16[128,512]{1,0:T(8,128)(2,1)} custom-call(bf16[128,512]{1,0:T(8,128)(2,1)} %queries.1, bf16[128,128]{1,0:T(8,128)(2,1)} %new_keys.1, bf16[128,128]{1,0:T(8,128)(2,1)} %new_values.1, bf16[2048,128]{1,0:T(8,128)(2,1)} %bitcast.8, bf16[2048,128]{1,0:T(8,128)(2,1)} %bitcast.9, s32[8,128]{1,0:T(8,128)} %bitcast.12, s32[16,128]{1,0:T(8,128)} %bitcast.11, ...), custom_call_target="tpu_custom_call" | custom-call | tf_op jit(solution)/shard_map/layer/pallas_call | solution.py:789
  119.5 1.6 %copy.18 = bf16[128,512]{1,0:T(8,128)(2,1)} copy(bf16[128,512]{1,0:T(8,128)(2,1)} %layer.1) | data formatting | bytes 262144

commit v5 on v4

--- a/solution.py
+++ b/solution.py
@@ -139,6 +139,8 @@
     moe_out,
     moe_in,
     moe_own,
+    scale_out,
+    scale_in,
     l_sems,
     s1,
     r1,
@@ -177,12 +179,16 @@
     m_recv,
     q_send,
     q_recv,
+    c_send,
+    c_recv,
+    c_own,
 ):
     dp = lax.axis_index("dp")
     mp = lax.axis_index("mp")
     z, y = dp // 4, lax.rem(dp, 4)
     scale = HD ** (-0.5)
-    peers = [lax.rem(dp + k, NDP) for k in range(1, NDP)]
+    offsets = ((2, 2), (2, 3), (3, 2), (2, 1), (1, 2), (2, 0), (0, 2), (3, 1), (1, 3), (3, 3), (1, 1), (3, 0), (0, 3), (1, 0), (0, 1))
+    peers = [lax.rem(z + a, 4) * 4 + lax.rem(y + b, 4) for a, b in offsets]
     mp_peers = [lax.rem(mp + k, 8) for k in range(1, 8)]
     x, c = mp // 2, lax.rem(mp, 2)
     xr, xo, xl = lax.rem(x + 1, 4), lax.rem(x + 2, 4), lax.rem(x + 3, 4)
@@ -350,26 +356,34 @@
         attn[DEC:, cols] = (num / den).astype(BF)
     loads[2].wait()
 
-    def project(t):
-        rows = slice(t * 64, (t + 1) * 64)
+    pieces = ((0, 32), (32, 32), (64, 64))
+
+    def piece_copy(i, k):
+        rows = pl.ds(*pieces[i])
+        return remote(
+            proj_part.at[k, rows], got.at[k, rows], ps.at[i, k], pr.at[i, k], {"mp": mp_peers[k]}
+        )
+
+    def project(i):
+        rows = pl.ds(*pieces[i])
         a = attn[rows, :]
         for k, p in enumerate(mp_peers):
             cols = pl.ds(pl.multiple_of(p * FW, FW), FW)
-            proj_part[t, k] = jnp.dot(a, proj_v[:, cols], preferred_element_type=F32).astype(BF)
-            go(remote(proj_part.at[t, k], got.at[t, k], ps.at[t, k], pr.at[t, k], {"mp": p}))
+            proj_part[k, rows] = jnp.dot(a, proj_v[:, cols], preferred_element_type=F32).astype(BF)
+            go(piece_copy(i, k))
         cols = pl.ds(pl.multiple_of(mp * FW, FW), FW)
         own = jnp.dot(a, proj_v[:, cols], preferred_element_type=F32)
         hidden[rows, :] = own + residual[rows, :].astype(F32)
 
-    def collect(t):
-        rows = slice(t * 64, (t + 1) * 64)
+    def collect(i):
+        rows = pl.ds(*pieces[i])
         total = hidden[rows, :]
         for k in range(7):
-            remote(proj_part.at[t, k], got.at[t, k], ps.at[t, k], pr.at[t, k], {"mp": mp_peers[k]}).wait_recv()
-            total = total + got[t, k].astype(F32)
+            piece_copy(i, k).wait_recv()
+            total = total + got[k, rows].astype(F32)
         hidden[rows, :] = total
 
-    project(1)
+    project(2)
 
     own_cols = jnp.zeros((64, 128), F32)
     lane64 = iota((64, 128), 1)
@@ -430,52 +444,51 @@
             owners[:, i * 256 : (i + 1) * 256], page_w[...], (((0,), (0,)), ((), ())), preferred_element_type=F32
         ).astype(BF)
 
-    def val_rows(p):
-        return val_out.at[pl.ds(pl.multiple_of(p * DEC, DEC), DEC), :]
-
     def swap_stat(k):
         p = peers[k]
         return remote(stat_out.at[p // 2], stat_in.at[k], ts.at[k], tr.at[k], {"dp": p})
 
-    def swap_val(k):
+    def swap_val(h, k):
         p = peers[k]
-        return remote(val_rows(p), val_in.at[k], vs.at[k], vr.at[k], {"dp": p})
+        rows = pl.ds(pl.multiple_of(p * DEC + h * 32, 32), 32)
+        return remote(val_out.at[rows, :], val_in.at[k, pl.ds(h * 32, 32), :], vs.at[h, k], vr.at[h, k], {"dp": p})
 
     for k in range(NDP - 1):
         go(swap_stat(k))
-        go(swap_val(k))
+        go(swap_val(0, k))
+    for k in range(NDP - 1):
+        go(swap_val(1, k))
 
     def square_copy(t, k):
         return remote(squares.at[t, 7], squares.at[t, k], q_send.at[t, k], q_recv.at[t, k], {"mp": mp_peers[k]})
 
-    def row_scales(t, rows):
+    def squares_start(t, rows):
         squares[t, 7] = square_sums(rows)
         for k in range(7):
             go(square_copy(t, k))
+
+    def squares_end(t):
         summed = squares[t, 7]
         for k in range(7):
             square_copy(t, k).wait_recv()
             summed = summed + squares[t, k]
         return as_columns(lax.rsqrt(summed / D + eps_norm))
 
-    def token_copy(t, k):
-        rows = tokens.at[x, pl.ds(t * 64, 64), :]
-        return remote(rows, rows, k_send.at[t, k], k_recv.at[t, k], x_peers[k])
+    def token_copy(i, k):
+        rows = tokens.at[x, pl.ds(*pieces[i]), :]
+        return remote(rows, rows, k_send.at[i, k], k_recv.at[i, k], x_peers[k])
 
     gain_rows = attn_gain[pl.ds(mp * 4, 4), :]
     gain_cols = jnp.concatenate([gain_rows[i : i + 1, :] for i in range(4)], axis=1)
-    nothing = jnp.zeros((64, FW), F32)
-
-    def finish(t):
-        mine = hidden[t * 64 : (t + 1) * 64, :]
-        scales = row_scales(t, jnp.concatenate([nothing, mine] if t else [mine, nothing], axis=0))
-        scales = scales[t * 64 : (t + 1) * 64, :]
-        tokens[x, t * 64 : (t + 1) * 64, :] = (mine * scales * gain_cols).astype(BF)
+
+    def finish(i):
+        rows = pl.ds(*pieces[i])
+        tokens[x, rows, :] = (hidden[rows, :] * gain_cols).astype(BF)
         for k in (0, 2, 1):
-            go(token_copy(t, k))
-
-    collect(1)
-    finish(1)
+            go(token_copy(i, k))
+
+    collect(2)
+    finish(2)
     for k in range(NDP - 1):
         swap_stat(k).wait_recv()
     stat_in[NDP - 1] = stat_out[dp // 2]
@@ -490,20 +503,22 @@
     inv = 1.0 / (jnp.sum(l_in * f_in, axis=0) + f_own)
     f_cols = to_columns((f_in * inv[None]).reshape(128, 128))
     own_f = to_columns(jnp.concatenate([f_own * inv, jnp.zeros((120, 128), F32)], axis=0))
-    nums = [own_f[:DEC, g : g + 1] * new_values[:DEC, :].astype(F32) for g in range(4)]
-    mine = val_out[pl.ds(pl.multiple_of(dp * DEC, DEC), DEC), :]
-    for k in range(NDP):
-        if k < NDP - 1:
-            swap_val(k).wait_recv()
-        v = (val_in[k] if k < NDP - 1 else mine).astype(F32)
+    for h in range(2):
+        rows = slice(h * 32, (h + 1) * 32)
+        nums = [own_f[rows, g : g + 1] * new_values[rows, :].astype(F32) for g in range(4)]
+        mine = val_out[pl.ds(pl.multiple_of(dp * DEC + h * 32, 32), 32), :]
+        for k in range(NDP):
+            if k < NDP - 1:
+                swap_val(h, k).wait_recv()
+            v = (val_in[k, rows] if k < NDP - 1 else mine).astype(F32)
+            for g in range(4):
+                nums[g] = nums[g] + v[:, g * HD : (g + 1) * HD] * f_cols[rows, 8 * k + g : 8 * k + g + 1]
         for g in range(4):
-            nums[g] = nums[g] + v[:, g * HD : (g + 1) * HD] * f_cols[:DEC, 8 * k + g : 8 * k + g + 1]
-    for g in range(4):
-        attn[:DEC, g * HD : (g + 1) * HD] = nums[g].astype(BF)
-    project(0)
-    collect(0)
-
-    finish(0)
+            attn[rows, g * HD : (g + 1) * HD] = nums[g].astype(BF)
+        project(h)
+    for h in range(2):
+        collect(h)
+        finish(h)
 
     def block(ch, h, owner):
         return x_all.at[ch, pl.ds(h * half, half), wide(owner)]
@@ -572,9 +587,9 @@
         return remote(x_all.at[2, :, c_cols], x_all.at[2, :, c_cols], p_send.at[2, 0], p_recv.at[2, 0], mate)
 
     def whole_start():
-        for t in range(2):
+        for i in range(3):
             for k in range(3):
-                token_copy(t, k).wait_recv()
+                token_copy(i, k).wait_recv()
         dispatch = picks[0, :, NA * 128 :] + picks[1, :, NA * 128 :]
         for chip in range(4):
             rows = lax.dot_general(
@@ -591,14 +606,43 @@
         whole_own().wait()
         go(whole_mate())
 
+    def scale_copy(k):
+        p = peers[k]
+        return remote(
+            scale_out.at[:, p // 2], scale_in.at[:, dp_rows, :], c_send.at[k], c_recv.at[k], {"dp": p}
+        )
+
+    def scale_own():
+        return pltpu.make_async_copy(scale_out.at[:, dp // 2], scale_in.at[:, dp_rows, :], c_own)
+
+    def scale_start():
+        scales = squares_end(0)[:, :128]
+        upper = scales.astype(BF)
+        lower = (scales - upper.astype(F32)).astype(BF)
+        both = jnp.where(iota((128, 128), 1) < 64, upper.astype(F32), lower.astype(F32)).astype(BF)
+        for ch in range(NCH):
+            rows = lax.dot_general(
+                dispatch[:, ch * 128 : (ch + 1) * 128], both, (((0,), (0,)), ((), ())), preferred_element_type=F32
+            ).astype(BF)
+            scale_out[ch] = rows.reshape(E, SL, 128)
+        scale_own().start()
+        for k in range(NDP - 1):
+            go(scale_copy(k))
+
+    def scale_end():
+        for k in range(NDP - 1):
+            scale_copy(k).wait_recv()
+        scale_own().wait()
+
     def hidden_send(ch):
         return remote(hid.at[ch, 0], hid.at[ch, 1], h_send.at[ch], h_recv.at[ch], mate)
 
     def gate_up(ch, n):
         cols = pl.ds(n * 256, 256)
         rows = x_all[ch]
-        g = jnp.dot(rows, wg_v[:, cols], preferred_element_type=F32)
-        u = jnp.dot(rows, wu_v[:, cols], preferred_element_type=F32)
+        scales = scale_in[ch, :, 0:1].astype(F32) + scale_in[ch, :, 64:65].astype(F32)
+        g = jnp.dot(rows, wg_v[:, cols], preferred_element_type=F32) * scales
+        u = jnp.dot(rows, wu_v[:, cols], preferred_element_type=F32) * scales
         hid[ch, 0, :, cols] = (g / (1.0 + jnp.exp(-g)) * u).astype(BF)
 
     def down(ch, chip):
@@ -721,7 +765,9 @@
         slice_own(ch).start()
         for k in range(NDP - 1):
             go(slice_copy(ch, k))
+    squares_start(0, hidden[...])
     spread_own(0)
+    scale_start()
     whole_start()
     spread_on(0)
     spread_own(1)
@@ -730,6 +776,7 @@
     for copy in w_copies[:16]:
         copy.wait()
     spread_end(0)
+    scale_end()
 
     gate_up(0, 0)
     spread_on(1)
@@ -776,7 +823,8 @@
     combine(1)
 
     mixed = moe_own[...]
-    result[...] = (mixed * row_scales(2, mixed) * final_gain[...]).astype(BF)
+    squares_start(1, mixed)
+    result[...] = (mixed * squares_end(1) * final_gain[...]).astype(BF)
     for copy in sent:
         copy.wait_send()
 
@@ -806,9 +854,9 @@
             V((8, 8, 128), F32),
             V((NDP, 8, 128), F32),
             V((128, FW), BF),
-            V((2, 7, 64, FW), BF),
-            V((2, 7, 64, FW), BF),
-            V((3, 8, 8, 128), F32),
+            V((7, 128, FW), BF),
+            V((7, 128, FW), BF),
+            V((2, 8, 8, 128), F32),
             V((128, FW), F32),
             V((2, 128, E * C), BF),
             V((NA, E, SL, FW), BF),
@@ -831,17 +879,19 @@
             V((3, 128, FW), BF),
             V((3, 128, FW), BF),
             V((128, FW), F32),
+            V((NCH, E, SL, 128), BF),
+            V((NCH, RC, 128), BF),
             DMA((4,)),
             DMA((2, 3)),
             DMA((2, 3)),
             DMA((2, 4, 3)),
             DMA((2, 4, 3)),
+            DMA((2, NDP - 1)),
+            DMA((2, NDP - 1)),
             DMA((NDP - 1,)),
             DMA((NDP - 1,)),
-            DMA((NDP - 1,)),
-            DMA((NDP - 1,)),
-            DMA((2, 7)),
-            DMA((2, 7)),
+            DMA((3, 7)),
+            DMA((3, 7)),
             DMA((20,)),
             DMA((3,)),
             DMA((NCH,)),
@@ -863,12 +913,15 @@
             DMA((NA, 2, 2)),
             DMA((NCH, NDP - 1)),
             DMA((NCH, NDP - 1)),
-            DMA((2, 3)),
-            DMA((2, 3)),
+            DMA((3, 3)),
+            DMA((3, 3)),
             DMA((3,)),
             DMA((3,)),
-            DMA((3, 7)),
-            DMA((3, 7)),
+            DMA((2, 7)),
+            DMA((2, 7)),
+            DMA((NDP - 1,)),
+            DMA((NDP - 1,)),
+            DMA,
         ],
         compiler_params=comm_params(collective_id),
         name="layer",

time: 121 us -> 114 us (0.942)
  Pallas kernels: 119 us -> 112 us
    pallas_call x1, Pallas kernels: 119 us -> 112 us  [layer(): pl.pallas_call(layer_kernel, out_shape=jax.ShapeDtypeStruct((128, FW), BF...]
where the time goes in v5:
time: 114 us
  Pallas kernels  112 us (98%)
  local copies, waits for them, and re-layouts  1.57 us (1%)
    pallas_call x1, Pallas kernels, layer(): pl.pallas_call(layer_kernel, out_shape=jax.ShapeDtypeStruct((128, FW), BF...  112 us

profile of v5, /device:TPU:1, one launch (start us, length us, event | category | flops | bytes accessed | tf_op | source)
XLA Modules:
  0.0 113.6 jit_solution(9256391739985775999)
XLA Ops:
  0.0 112.1 %layer.1 = bf16[128,512]{1,0:T(8,128)(2,1)} custom-call(bf16[128,512]{1,0:T(8,128)(2,1)} %queries.1, bf16[128,128]{1,0:T(8,128)(2,1)} %new_keys.1, bf16[128,128]{1,0:T(8,128)(2,1)} %new_values.1, bf16[2048,128]{1,0:T(8,128)(2,1)} %bitcast.8, bf16[2048,128]{1,0:T(8,128)(2,1)} %bitcast.9, s32[8,128]{1,0:T(8,128)} %bitcast.12, s32[16,128]{1,0:T(8,128)} %bitcast.11, ...), custom_call_target="tpu_custom_call" | custom-call | tf_op jit(solution)/shard_map/layer/pallas_call | solution.py:837
  112.1 1.6 %copy.18 = bf16[128,512]{1,0:T(8,128)(2,1)} copy(bf16[128,512]{1,0:T(8,128)(2,1)} %layer.1) | data formatting | bytes 262144

commit v6 on v5

--- a/solution.py
+++ b/solution.py
@@ -189,7 +189,8 @@
     scale = HD ** (-0.5)
     offsets = ((2, 2), (2, 3), (3, 2), (2, 1), (1, 2), (2, 0), (0, 2), (3, 1), (1, 3), (3, 3), (1, 1), (3, 0), (0, 3), (1, 0), (0, 1))
     peers = [lax.rem(z + a, 4) * 4 + lax.rem(y + b, 4) for a, b in offsets]
-    mp_peers = [lax.rem(mp + k, 8) for k in range(1, 8)]
+    mp_offsets = ((2, 0), (2, 1), (1, 0), (3, 0), (1, 1), (3, 1), (0, 1))
+    mp_peers = [lax.rem(mp // 2 + a, 4) * 2 + lax.rem(mp + b, 2) for a, b in mp_offsets]
     x, c = mp // 2, lax.rem(mp, 2)
     xr, xo, xl = lax.rem(x + 1, 4), lax.rem(x + 2, 4), lax.rem(x + 3, 4)
     mr, mo, ml = xr * 2 + c, xo * 2 + c, xl * 2 + c
@@ -270,11 +271,11 @@
             q_half(owner, h), q_half(owner, h), s2.at[h, j, k - 1], r2.at[h, j, k - 1], {"dp": group(h, 0, k)}
         )
 
-    for k in (1, 3, 2):
+    for k in (2, 1, 3):
         for h in range(2):
             go(first(h, k))
-    for h in range(2):
-        for k in range(1, 4):
+    for k in (2, 1, 3):
+        for h in range(2):
             go(second(h, 0, k))
     mate_w = []
     for j in range(4):
@@ -311,7 +312,7 @@
     for k in range(1, 4):
         for h in range(2):
             remote(q_half(dp, h), q_half(group(h, -k, 0), h), s1.at[h, k - 1], r1.at[h, k - 1], {"dp": peers[0]}).wait_recv()
-            for kk in range(1, 4):
+            for kk in (2, 1, 3):
                 go(second(h, k, kk))
 
     begin = jnp.zeros((128, 128), F32)
@@ -484,7 +485,7 @@
     def finish(i):
         rows = pl.ds(*pieces[i])
         tokens[x, rows, :] = (hidden[rows, :] * gain_cols).astype(BF)
-        for k in (0, 2, 1):
+        for k in (1, 0, 2):
             go(token_copy(i, k))
 
     collect(2)

time: 114 us -> 114 us (level)
  no operation moved by 1% of the time
where the time goes in v6:
time: 114 us
  Pallas kernels  112 us (98%)
  local copies, waits for them, and re-layouts  1.57 us (1%)
    pallas_call x1, Pallas kernels, layer(): pl.pallas_call(layer_kernel, out_shape=jax.ShapeDtypeStruct((128, FW), BF...  112 us

profile of v6, /device:TPU:1, one launch (start us, length us, event | category | flops | bytes accessed | tf_op | source)
XLA Modules:
  0.0 114.0 jit_solution(7536847156953534301)
XLA Ops:
  0.0 112.4 %layer.1 = bf16[128,512]{1,0:T(8,128)(2,1)} custom-call(bf16[128,512]{1,0:T(8,128)(2,1)} %queries.1, bf16[128,128]{1,0:T(8,128)(2,1)} %new_keys.1, bf16[128,128]{1,0:T(8,128)(2,1)} %new_values.1, bf16[2048,128]{1,0:T(8,128)(2,1)} %bitcast.8, bf16[2048,128]{1,0:T(8,128)(2,1)} %bitcast.9, s32[8,128]{1,0:T(8,128)} %bitcast.12, s32[16,128]{1,0:T(8,128)} %bitcast.11, ...), custom_call_target="tpu_custom_call" | custom-call | tf_op jit(solution)/shard_map/layer/pallas_call | solution.py:838
  112.4 1.6 %copy.18 = bf16[128,512]{1,0:T(8,128)(2,1)} copy(bf16[128,512]{1,0:T(8,128)(2,1)} %layer.1) | data formatting | bytes 262144
